TPU v7x, 32 devices: a whole 2x2x4 slice. The times are simulated.
32 devices in a mesh: seq: 8 (over z, y), tp: 4 (over x, core).
Axes of the slice: x: 2, y: 2, z: 4, core: 2. Of those that a mesh axis runs over, the one named last changes fastest.
Arguments:
- prefill_tokens: bfloat16 [4096, 2304], P('seq'), may hold values from -6 to 6
- decode_tokens: bfloat16 [64, 2304], P('seq'), may hold values from -6 to 6
- attention_gain: float32 [2304], replicated, may hold values from 0.5 to 1.5
- qkv_weight: bfloat16 [2304, 3, 2304], P(None, None, 'tp'), may hold values from -0.125 to 0.125
- out_weight: bfloat16 [2304, 2304], P('tp'), may hold values from -0.375 to 0.375
- feedforward_gain: float32 [2304], replicated, may hold values from 0.5 to 1.5
- prefill_cache: bfloat16 [8, 2, 1024, 2304], P('seq', None, None, 'tp'), may hold values from -420 to 420
- prefill_offsets: int32 [8], P('seq'), may hold values from 0 to 1024, as said below
- decode_cache: bfloat16 [64, 2, 256, 2304], P('seq', None, None, 'tp'), may hold values from -420 to 420
- decode_lengths: int32 [64], P('seq'), may hold values from 1 to 256, as said below
- request_slot: int32 [64], replicated, may hold values from 0 to 63, each once
Outputs:
- prefill_hidden: bfloat16 [4096, 2304], P('seq')
- decode_hidden: bfloat16 [64, 2304], P('seq')
- prefill_normed: bfloat16 [4096, 2304], P('seq')
- decode_normed: bfloat16 [64, 2304], P('seq')
Inputs may be any that keep to these rules, and one draw needn't show every extreme that they name: `request_slot`: each slot is named by exactly one request. `decode_lengths`: some slot holds exactly 256 positions. `prefill_offsets`: some request has exactly 1024 cached positions.
All inputs are finite; a program needn't handle non-finite values.
Results may differ from a plain program's by a relative error of at most 0.014.
The roundings to bfloat16 on the way count: a program that leaves them out, or rounds other values in their place, can miss the bound.
Values may be sent and summed in bfloat16 or wider, within the bound.
A program may use at most 128 MiB of HBM per device.

v0:
```python
import math

import jax
import jax.numpy as jnp
from jax import lax
from jax.sharding import PartitionSpec as P

HEAD = 64


RMS_EPSILON = 1e-05
ROPE_BASE = 10000.0
NEGATIVE = -1e30


def rms_norm(stream, gain):
    widened = stream.astype(jnp.float32)
    inverse = lax.rsqrt(jnp.mean(widened * widened, axis=-1, keepdims=True) + RMS_EPSILON)
    return widened * inverse * gain


def rotate(vectors, positions):
    half_dim = vectors.shape[-1] // 2
    exponent = jnp.arange(half_dim, dtype=jnp.float32) * (2.0 / vectors.shape[-1])
    frequency = ROPE_BASE ** (-exponent)
    angles = positions[:, None] * frequency[None, :]
    cosine = jnp.cos(angles)[:, None, :]
    sine_part = jnp.sin(angles)[:, None, :]
    first_half = vectors[..., :half_dim]
    second_half = vectors[..., half_dim:]
    return jnp.concatenate(
        [
            first_half * cosine - second_half * sine_part,
            second_half * cosine + first_half * sine_part,
        ],
        axis=-1,
    )


def prefill_attention(block_rows, cache_pair, offset, head_count):
    span_rows = block_rows.shape[0]
    cache_len = cache_pair.shape[1]
    score_scale = 1.0 / math.sqrt(HEAD)
    positions = offset.astype(jnp.float32) + jnp.arange(span_rows, dtype=jnp.float32)
    queries = rotate(
        block_rows[:, 0].reshape(span_rows, head_count, HEAD).astype(jnp.float32), positions
    ).astype(jnp.bfloat16)
    new_keys = rotate(
        block_rows[:, 1].reshape(span_rows, head_count, HEAD).astype(jnp.float32), positions
    ).astype(jnp.bfloat16)
    new_values = block_rows[:, 2].reshape(span_rows, head_count, HEAD)
    cache_keys = cache_pair[0].reshape(cache_len, head_count, HEAD)
    cache_values = cache_pair[1].reshape(cache_len, head_count, HEAD)
    cache_scores = (
        jnp.einsum("qhe,khe->hqk", queries, cache_keys, preferred_element_type=jnp.float32)
        * score_scale
    )
    span_scores = (
        jnp.einsum("qhe,khe->hqk", queries, new_keys, preferred_element_type=jnp.float32)
        * score_scale
    )
    cache_visible = (jnp.arange(cache_len, dtype=jnp.int32) < offset)[None, None, :]
    causal = (
        jnp.arange(span_rows, dtype=jnp.int32)[None, :]
        <= jnp.arange(span_rows, dtype=jnp.int32)[:, None]
    )[None]
    cache_scores = jnp.where(cache_visible, cache_scores, NEGATIVE)
    span_scores = jnp.where(causal, span_scores, NEGATIVE)
    row_peak = jnp.maximum(
        jnp.max(cache_scores, axis=-1, keepdims=True), jnp.max(span_scores, axis=-1, keepdims=True)
    )
    cache_exp = jnp.exp(cache_scores - row_peak)
    span_exp = jnp.exp(span_scores - row_peak)
    denominator = jnp.sum(cache_exp, axis=-1, keepdims=True) + jnp.sum(
        span_exp, axis=-1, keepdims=True
    )
    cache_weights = (cache_exp / denominator).astype(jnp.bfloat16)
    span_weights = (span_exp / denominator).astype(jnp.bfloat16)
    attended = jnp.einsum(
        "hqk,khe->qhe", cache_weights, cache_values, preferred_element_type=jnp.float32
    )
    attended = attended + jnp.einsum(
        "hqk,khe->qhe", span_weights, new_values, preferred_element_type=jnp.float32
    )
    return attended.reshape(span_rows, head_count * HEAD).astype(jnp.bfloat16)


def decode_attention(routed, cache_block, lengths, head_count):
    slot_count = routed.shape[0]
    cache_len = cache_block.shape[2]
    score_scale = 1.0 / math.sqrt(HEAD)
    positions = lengths.astype(jnp.float32)
    queries = rotate(
        routed[:, 0].reshape(slot_count, head_count, HEAD).astype(jnp.float32), positions
    ).astype(jnp.bfloat16)
    new_keys = rotate(
        routed[:, 1].reshape(slot_count, head_count, HEAD).astype(jnp.float32), positions
    ).astype(jnp.bfloat16)
    new_values = routed[:, 2].reshape(slot_count, head_count, HEAD)
    cache_keys = cache_block[:, 0].reshape(slot_count, cache_len, head_count, HEAD)
    cache_values = cache_block[:, 1].reshape(slot_count, cache_len, head_count, HEAD)
    cache_scores = (
        jnp.einsum("she,skhe->shk", queries, cache_keys, preferred_element_type=jnp.float32)
        * score_scale
    )
    self_scores = (
        jnp.einsum("she,she->sh", queries, new_keys, preferred_element_type=jnp.float32)
        * score_scale
    )
    visible = (jnp.arange(cache_len, dtype=jnp.int32)[None, :] < lengths[:, None])[:, None, :]
    cache_scores = jnp.where(visible, cache_scores, NEGATIVE)
    row_peak = jnp.maximum(jnp.max(cache_scores, axis=-1), self_scores)
    cache_exp = jnp.exp(cache_scores - row_peak[..., None])
    self_exp = jnp.exp(self_scores - row_peak)
    denominator = jnp.sum(cache_exp, axis=-1) + self_exp
    cache_weights = (cache_exp / denominator[..., None]).astype(jnp.bfloat16)
    self_weights = (self_exp / denominator).astype(jnp.bfloat16)
    attended = jnp.einsum(
        "shk,skhe->she", cache_weights, cache_values, preferred_element_type=jnp.float32
    )
    attended = attended + self_weights.astype(jnp.float32)[..., None] * new_values.astype(
        jnp.float32
    )
    return attended.reshape(slot_count, head_count * HEAD).astype(jnp.bfloat16)


def local(
    prefill_tokens,
    decode_tokens,
    attention_gain,
    qkv_weight,
    out_weight,
    feedforward_gain,
    prefill_cache,
    prefill_offsets,
    decode_cache,
    decode_lengths,
    request_slot,
):
    span_rows = prefill_tokens.shape[0]
    decode_rows = decode_tokens.shape[0]
    model_width = prefill_tokens.shape[1]
    local_width = out_weight.shape[0]
    head_count = local_width // HEAD
    tokens_all = jnp.concatenate([prefill_tokens, decode_tokens], axis=0)
    normed_in = rms_norm(tokens_all, attention_gain).astype(jnp.bfloat16)
    projected = jnp.dot(
        normed_in,
        qkv_weight.reshape(model_width, 3 * local_width),
        preferred_element_type=jnp.float32,
    ).astype(jnp.bfloat16)
    projected = projected.reshape(-1, 3, local_width)
    prefill_block = projected[:span_rows]
    decode_block = projected[span_rows:]
    seq_rank = lax.axis_index("seq")
    own_slots = seq_rank * decode_rows + jnp.arange(decode_rows, dtype=jnp.int32)
    arrived = lax.all_gather(decode_block, "seq", axis=0, tiled=True)
    picker = (request_slot[None, :] == own_slots[:, None]).astype(jnp.bfloat16)
    routed = jnp.einsum("sr,rcw->scw", picker, arrived, preferred_element_type=jnp.float32).astype(
        jnp.bfloat16
    )
    slot_results = decode_attention(routed, decode_cache, decode_lengths, head_count)
    prefill_attended = prefill_attention(
        prefill_block, prefill_cache[0], prefill_offsets[0], head_count
    )
    my_slots = lax.dynamic_slice_in_dim(request_slot, seq_rank * decode_rows, decode_rows)
    shard_piece = lax.all_gather(slot_results, "seq", axis=0, tiled=True)
    slot_ids = jnp.arange(shard_piece.shape[0], dtype=jnp.int32)
    picker = (my_slots[:, None] == slot_ids[None, :]).astype(jnp.bfloat16)
    returned = jnp.dot(picker, shard_piece, preferred_element_type=jnp.float32).astype(jnp.bfloat16)
    attended_all = jnp.concatenate([prefill_attended, returned], axis=0)
    partial_value = jnp.dot(attended_all, out_weight, preferred_element_type=jnp.float32)
    combined = lax.psum(partial_value.astype(jnp.bfloat16), "tp").astype(jnp.float32)
    hidden = (tokens_all.astype(jnp.float32) + combined).astype(jnp.bfloat16)
    normed = rms_norm(hidden, feedforward_gain).astype(jnp.bfloat16)
    return (hidden[:span_rows], hidden[span_rows:], normed[:span_rows], normed[span_rows:])


def solution(mesh):
    placed = (
        P("seq", None),
        P("seq", None),
        P(),
        P(None, None, "tp"),
        P("tp", None),
        P(),
        P("seq", None, None, "tp"),
        P("seq"),
        P("seq", None, None, "tp"),
        P("seq"),
        P(),
    )
    return jax.shard_map(
        local,
        mesh=mesh,
        in_specs=placed,
        out_specs=(P("seq", None), P("seq", None), P("seq", None), P("seq", None)),
        check_vma=False,
    )
```

profile of v0, /device:TPU:0, one launch (start us, length us, event | category | flops | bytes accessed | tf_op | source)
XLA Modules:
  0.0 215.5 jit_solution(18062923695454391334)
XLA Ops:
  8.8 2.4 %fusion.8 = f32[520]{0:T(1024)S(1)} fusion(bf16[8,2304]{1,0:T(8,128)(2,1)} %param.12, bf16[512,2304]{1,0:T(8,128)(2,1)} %param.11), kind=kLoop, calls=%fused_computation.19 | loop fusion | flops 7187960 | bytes 2398240 | tf_op jit(solution)/shard_map/reduce_sum | solution.py:18
  11.2 8.6 %convolution_convert_fusion.1 = bf16[520,1728]{1,0:T(8,128)(2,1)S(1)} fusion(bf16[2304,1728]{0,1:T(8,128)(2,1)} %bitcast.71, f32[2304]{0:T(1024)} %param.13, f32[520]{0:T(1024)S(1)} %add_rsqrt_fusion.1, bf16[8,2304]{1,0:T(8,128)(2,1)} %param.12, bf16[512,2304]{1,0:T(8,128)(2,1)} %param.11), kind=kOutput, calls=%fused_computation.25 | convolution fusion | flops 4149849600 | bytes 12167200 | tf_op jit(solution)/shard_map/dot_general | solution.py:147
  19.8 1.4 slice.106
  21.3 2.5 %fusion.55 = (bf16[8,1,256,576]{2,3,1,0:T(8,128)(2,1)}, bf16[8,1,256,576]{2,3,1,0:T(8,128)(2,1)}) fusion(bf16[8,2,256,576]{2,3,1,0:T(8,128)(2,1)S(1)} %bitcast.64), kind=kLoop, calls=%fused_computation.103 | loop fusion | bytes 9437184 | tf_op jit(solution)/shard_map/slice | solution.py:100
  23.9 32.5 %all_gather.6 = bf16[64,3,576]{2,0,1:T(8,128)(2,1)S(1)} all-gather(bf16[8,3,576]{2,0,1:T(8,128)(2,1)S(1)} %copy.25), channel_id=1, replica_groups=mesh['seq'=8,'tp'=4] {'seq'}, dimensions={0}, use_global_device_ids=true | all-gather | bytes 248832 | tf_op jit(solution)/shard_map/all_gather | solution.py:157
  57.4 2.1 fusion.35
  60.1 2.4 %fusion.29 = f32[8,9,1,64]{3,2,1,0:T(1,128)S(1)} fusion(bf16[8,256,9,64]{1,3,2,0:T(8,128)(2,1)} %bitcast.68, bf16[8,9,256,1]{2,0,1,3:T(8,128)(2,1)S(1)} %fusion.37), kind=kOutput, calls=%fused_computation.53 | convolution fusion | flops 2359296 | bytes 2414592 | tf_op jit(solution)/shard_map/shk,skhe->she/dot_general | solution.py:118
  62.6 30.5 %all_gather.7 = bf16[64,576]{1,0:T(8,128)(2,1)S(1)} all-gather(bf16[8,576]{1,0:T(8,128)(2,1)S(1)} %convert_element_type.124), channel_id=1, replica_groups=mesh['seq'=8,'tp'=4] {'seq'}, dimensions={0}, use_global_device_ids=true | all-gather | bytes 82944 | tf_op jit(solution)/shard_map/all_gather | solution.py:167
  94.2 3.2 %fusion.56 = (bf16[1,1,1024,576]{2,3,1,0:T(8,128)(2,1)}, bf16[1,1,1024,576]{2,3,1,0:T(8,128)(2,1)}) fusion(bf16[1,2,1024,576]{2,3,1,0:T(8,128)(2,1)} %param.17), kind=kLoop, calls=%fused_computation.104 | loop fusion | bytes 4718592 | tf_op jit(solution)/shard_map/slice | solution.py:52
  98.1 4.0 %copy.23 = bf16[512,1728]{0,1:T(8,128)(2,1)} copy(bf16[512,1728]{1,0:T(8,128)(2,1)} %slice.106) | data formatting | bytes 3538944 | tf_op jit(solution)/shard_map/slice | solution.py:153
  102.1 2.4 %fusion.57 = (bf16[512,1,576]{0,2,1:T(8,128)(2,1)}, bf16[512,1,576]{0,2,1:T(8,128)(2,1)S(1)}, bf16[512,1,576]{0,2,1:T(8,128)(2,1)S(1)}) fusion(bf16[512,3,576]{0,2,1:T(8,128)(2,1)} %bitcast.62), kind=kLoop, calls=%fused_computation.105 | loop fusion | bytes 3538944 | tf_op jit(solution)/shard_map/slice | solution.py:51
  104.5 1.2 convert.40
  106.1 1.6 subtract_convert_fusion
  107.7 2.8 %fusion = (f32[9,512]{1,0:T(8,128)S(1)}, f32[9,512,1024]{2,1,0:T(8,128)S(1)}) fusion(pred[1024]{0:T(1024)(128)(4,1)S(1)} %iota_compare_fusion.3, bf16[1024,9,64]{0,2,1:T(8,128)(2,1)S(1)} %bitcast.65, bf16[512,9,32]{0,2,1:T(8,128)(2,1)S(1)} %get-tuple-element.17, bf16[512,9,32]{0,2,1:T(8,128)(2,1)S(1)} %get-tuple-element.18), kind=kOutput, calls=%fused_computation.3 | convolution fusion | flops 619310592 | bytes 20663296 | tf_op jit(solution)/shard_map/qhe,khe->hqk/dot_general | solution.py:55
  110.5 5.3 %fusion.3 = (f32[9,512]{1,0:T(8,128)S(1)}, f32[9,512,512]{1,2,0:T(8,128)}) fusion(pred[512,512]{0,1:T(8,128)(4,1)S(1)} %iota_compare_fusion, bf16[512,9,32]{0,2,1:T(8,128)(2,1)S(1)} %get-tuple-element.14, bf16[512,9,32]{0,2,1:T(8,128)(2,1)S(1)} %get-tuple-element.13, bf16[512,9,32]{0,2,1:T(8,128)(2,1)S(1)} %get-tuple-element.17, ...), kind=kOutput, calls=%fused_computation.9 | convolution fusion | flops 311422464 | bytes 10897408 | tf_op jit(solution)/shard_map/qhe,khe->hqk/dot_general | solution.py:59
  115.8 4.5 %fusion.1 = f32[9,512]{1,0:T(8,128)S(1)} fusion(f32[9,512,1024]{2,1,0:T(8,128)S(1)} %get-tuple-element.35, f32[9,512]{1,0:T(8,128)S(1)} %max.11, pred[1024]{0:T(1024)(128)(4,1)S(1)} %iota_compare_fusion.3), kind=kLoop, calls=%fused_computation.4 | loop fusion | flops 18869760 | bytes 18912256 | tf_op jit(solution)/shard_map/reduce_sum | solution.py:74
  120.4 5.6 %fusion.4 = f32[9,512]{1,0:T(8,128)S(1)} fusion(f32[9,512,512]{1,2,0:T(8,128)} %get-tuple-element.37, f32[9,512]{1,0:T(8,128)S(1)} %max.11, pred[512,512]{0,1:T(8,128)(4,1)S(1)} %iota_compare_fusion), kind=kLoop, calls=%fused_computation.10 | loop fusion | flops 9432576 | bytes 9736192 | tf_op jit(solution)/shard_map/reduce_sum | solution.py:74
  126.0 7.1 %fusion.16 = f32[512,9,64]{0,2,1:T(8,128)} fusion(bf16[1024,9,64]{0,2,1:T(8,128)(2,1)} %bitcast.69, f32[9,512,1024]{2,1,0:T(8,128)S(1)} %get-tuple-element.35, f32[9,512]{1,0:T(8,128)S(1)} %add.78, f32[9,512]{1,0:T(8,128)S(1)} %max.11, pred[1024]{0:T(1024)(128)(4,1)S(1)} %iota_compare_fusion.3), kind=kOutput, calls=%fused_computation.29 | convolution fusion | flops 627572736 | bytes 21271552 | tf_op jit(solution)/shard_map/hqk,khe->qhe/dot_general | solution.py:79
  133.1 6.0 %fusion.19 = bf16[512,9,64]{0,2,1:T(8,128)(2,1)S(1)} fusion(f32[512,9,64]{0,2,1:T(8,128)} %fusion.16, bf16[512,9,64]{0,2,1:T(8,128)(2,1)S(1)} %bitcast.70, f32[9,512,512]{1,2,0:T(8,128)} %get-tuple-element.37, f32[9,512]{1,0:T(8,128)S(1)} %add.78, f32[9,512]{1,0:T(8,128)S(1)} %max.11, pred[512,512]{0,1:T(8,128)(4,1)S(1)} %iota_compare_fusion), kind=kOutput, calls=%fused_computation.32 | convolution fusion | flops 314376192 | bytes 12095488 | tf_op jit(solution)/shard_map/hqk,khe->qhe/dot_general | solution.py:82
  139.1 3.5 %convolution_convert_fusion = bf16[520,2304]{1,0:T(8,128)(2,1)} fusion(bf16[576,2304]{1,0:T(8,128)(2,1)S(1)} %copy-done, bf16[8,576]{0,1:T(8,128)(2,1)S(1)} %copy-done.4, bf16[512,576]{0,1:T(8,128)(2,1)S(1)} %bitcast.72), kind=kOutput, calls=%fused_computation.24 | convolution fusion | flops 1382584320 | bytes 5649408 | tf_op jit(solution)/shard_map/dot_general | solution.py:172
  142.6 57.6 %all-reduce.2.cloned.1.call-done = bf16[520,2304]{1,0:T(8,128)(2,1)} async-done(((bf16[520,2304]{1,0:T(8,128)(2,1)}), bf16[520,2304]{1,0:T(8,128)(2,1)}) %all-reduce.2.cloned.1.call-update) | async-done | bytes 2396176 | tf_op jit(solution)/shard_map/psum | solution.py:173
  200.2 3.4 %fusion.5 = (f32[520]{0:T(1024)S(1)}, bf16[520,2304]{1,0:T(8,128)(2,1)S(1)}) fusion(bf16[520,2304]{1,0:T(8,128)(2,1)} %all-reduce.2.cloned.1.call-done, bf16[8,2304]{1,0:T(8,128)(2,1)S(1)} %copy-done.3, bf16[512,2304]{1,0:T(8,128)(2,1)} %param.11), kind=kLoop, calls=%fused_computation.16 | loop fusion | flops 11980280 | bytes 7190560 | tf_op jit(solution)/shard_map/reduce_sum | solution.py:18
  203.6 1.6 slice.122
  206.4 1.6 slice.124
  (61 shorter events, 6.9 us)
Async XLA Ops:
  7.2 131.9 %copy-start = (bf16[576,2304]{1,0:T(8,128)(2,1)S(1)}, bf16[576,2304]{1,0:T(8,128)(2,1)}, u32[]{:S(2)}) copy-start(bf16[576,2304]{1,0:T(8,128)(2,1)} %param.15) | copy-start | bytes 7962628
  7.2 193.0 %all-reduce.2.cloned.1.call-start = ((), (), s32[]{:S(2)}) async-start(), calls=%async_computation | async-start | bytes 4792320 | tf_op jit(solution)/shard_map/psum | solution.py:173
  8.8 12.5 %slice-start = ((s8[4718592]{0:T(1024)(128)(4,1)}), s8[4194304]{0:T(1024)(128)(4,1)S(1)}, s32[]{:S(2)}) async-start(s8[4718592]{0:T(1024)(128)(4,1)} %bitcast.63), calls=%async_computation.1 | async-start | bytes 8388608
  11.2 10.1 %slice-start.1 = ((s8[4718592]{0:T(1024)(128)(4,1)}), s8[524288]{0:T(1024)(128)(4,1)S(1)}, s32[]{:S(2)}) async-start(s8[4718592]{0:T(1024)(128)(4,1)} %bitcast.63), calls=%async_computation.2 | async-start | bytes 1048576
  21.3 35.1 %copy-start.6 = (s32[64]{0:T(128)S(1)}, s32[64]{0:T(128)}, u32[]{:S(2)}) copy-start(s32[64]{0:T(128)} %param.21) | copy-start | bytes 772
  105.6 2.1 copy-start.1
  126.0 7.1 %copy-start.2 = (bf16[512,1,576]{0,2,1:T(8,128)(2,1)S(1)}, bf16[512,1,576]{0,2,1:T(8,128)(2,1)}, u32[]{:S(2)}) copy-start(bf16[512,1,576]{0,2,1:T(8,128)(2,1)} %get-tuple-element.10) | copy-start | bytes 1769476
  133.1 6.0 %copy-start.4 = (bf16[8,576]{0,1:T(8,128)(2,1)S(1)}, bf16[8,576]{0,1:T(8,128)(2,1)}, u32[]{:S(2)}) copy-start(bf16[8,576]{0,1:T(8,128)(2,1)} %copy.27) | copy-start | bytes 27652
  139.1 61.1 %copy-start.3 = (bf16[8,2304]{1,0:T(8,128)(2,1)S(1)}, bf16[8,2304]{1,0:T(8,128)(2,1)}, u32[]{:S(2)}) copy-start(bf16[8,2304]{1,0:T(8,128)(2,1)} %param.12) | copy-start | bytes 110596
  142.6 63.2 %copy-start.5 = (f32[2304]{0:T(1024)S(1)}, f32[2304]{0:T(1024)}, u32[]{:S(2)}) copy-start(f32[2304]{0:T(1024)} %param.16) | copy-start | bytes 27652
Sparse Core Ops, SparseCore 0:
  142.8 57.4 all-reduce.1
where the time goes:
time: 216 us; the launch traced here: 215 us
  blocking collectives  63.1 us (29%)
  waiting for transfers between devices  57.6 us (27%)
  matrix products  38.1 us (18%)
  other arithmetic  22.4 us (10%)
  local copies, waits for them, and re-layouts  19.3 us (9%)
  between operations  15 us (7%)
    psum x1, waiting for transfers between devices, local(): lax.psum(partial_value.astype(jnp.bfloat16), 'tp').astype(jnp.float32)  57.6 us
    all_gather x1, blocking collectives, local(): arrived = lax.all_gather(decode_block, 'seq', axis=0, tiled=True)  32.5 us
    all_gather x1, blocking collectives, local(): shard_piece = lax.all_gather(slot_results, 'seq', axis=0, tiled=True)  30.5 us
    dot_general x1, matrix products, local(): jnp.dot(normed_in, qkv_weight.reshape(model_width, 3 * local_width), pref...  8.62 us
    dot_general x1, matrix products, prefill_attention(): jnp.einsum('hqk,khe->qhe', cache_weights, cache_values, preferred_element...  7.07 us
    dot_general x1, matrix products, prefill_attention(): jnp.einsum('hqk,khe->qhe', span_weights, new_values, preferred_element_ty...  6 us
    reduce_sum x2, other arithmetic, rms_norm(): jnp.mean(widened * widened, axis=-1, keepdims=True) + RMS_EPSILON  5.77 us
    reduce_sum x1, other arithmetic, prefill_attention(): jnp.sum(span_exp, axis=-1, keepdims=True)  5.61 us
  transfers between devices with their start and end apart: 1, of which 1 were waited for; matrix products, arithmetic and copies ran while one was open for 0% of the time, Pallas kernels for 0%

commit v1 on v0

v1 whole, which is shorter than its diff:
```python
import functools

import jax
import jax.numpy as jnp
from jax import lax
from jax.experimental import pallas as pl
from jax.experimental.pallas import tpu as pltpu
from jax.sharding import PartitionSpec as P

HEAD = 64
HALF = HEAD // 2
RMS_EPSILON = 1e-05
ROPE_BASE = 10000.0
NEGATIVE = -1e30
MIB = 1 << 20
F32, BF16 = jnp.float32, jnp.bfloat16
MESH = pl.DeviceIdType.MESH
VMEM = pltpu.VMEM
VSPEC = pl.BlockSpec(memory_space=pltpu.VMEM)
ASPEC = pl.BlockSpec(memory_space=pl.ANY)


def dot(a, b, ca, cb):
    return lax.dot_general(a, b, (((ca,), (cb,)), ((), ())), preferred_element_type=F32)


def rms_rows(x, gain):
    inverse = lax.rsqrt(jnp.mean(x * x, axis=-1, keepdims=True) + RMS_EPSILON)
    return (x * inverse * gain).astype(BF16)


def rotate_columns(x, cosine, sine, scale):
    pieces = []
    for head in range(x.shape[0] // HEAD):
        a = x[head * HEAD : head * HEAD + HALF]
        b = x[head * HEAD + HALF : (head + 1) * HEAD]
        pieces.append(a * cosine - b * sine)
        pieces.append(b * cosine + a * sine)
    turned = jnp.concatenate(pieces, axis=0).astype(BF16)
    return turned if scale is None else (turned.astype(F32) * scale).astype(BF16)


def project_kernel(tok_ref, dtok_ref, gain_ref, w_ref, cos_ref, sin_ref, out_ref, dec_ref, normed, dnormed):
    part = pl.program_id(0)
    rows = tok_ref.shape[0]

    @pl.when(part == 0)
    def _():
        @pl.loop(0, rows // 64)
        def _(i):
            span = pl.ds(pl.multiple_of(i * 64, 64), 64)
            normed[span, :] = rms_rows(tok_ref[span, :].astype(F32), gain_ref[...])

        dnormed[...] = rms_rows(dtok_ref[...].astype(F32), gain_ref[...])

    w = w_ref[0]
    product = dot(w, normed[...], 1, 1).astype(BF16)
    dec_ref[0] = dot(dnormed[...], w, 1, 1).astype(BF16)

    @pl.when(part == 2)
    def _():
        out_ref[0] = product

    @pl.when(part < 2)
    def _():
        scale = jnp.where(part == 0, 0.125, 1.0)
        out_ref[0] = rotate_columns(product.astype(F32), cos_ref[...], sin_ref[...], scale)


def project(tokens, decode_tokens, gain, w, cosine, sine):
    rows, width = tokens.shape
    drows = decode_tokens.shape[0]
    local = w.shape[1]
    whole = lambda shape: pl.BlockSpec(shape, lambda i: (0,) * len(shape), pipeline_mode=pl.Buffered(1))
    return pl.pallas_call(
        project_kernel,
        grid=(3,),
        in_specs=[
            whole((rows, width)),
            whole((drows, width)),
            whole((1, width)),
            pl.BlockSpec((1, local, width), lambda i: (i, 0, 0)),
            whole((HALF, rows)),
            whole((HALF, rows)),
        ],
        out_specs=[
            pl.BlockSpec((1, local, rows), lambda i: (i, 0, 0)),
            pl.BlockSpec((1, drows, local), lambda i: (i, 0, 0)),
        ],
        out_shape=[
            jax.ShapeDtypeStruct((3, local, rows), BF16),
            jax.ShapeDtypeStruct((3, drows, local), BF16),
        ],
        scratch_shapes=[VMEM((rows, width), BF16), VMEM((drows, width), BF16)],
        compiler_params=pltpu.CompilerParams(vmem_limit_bytes=40 * MIB),
        name="project",
    )(tokens, decode_tokens, gain, w, cosine, sine)


def decode_kernel(
    n, dec_ref, pick_ref, back_ref, cos_ref, sin_ref, bias_ref, cache_hbm, out_ref,
    arrived, results, cache, cache_sem, send1, recv1, send2, recv2,
):
    slots = dec_ref.shape[1]
    local = dec_ref.shape[2]
    heads = local // HEAD
    rows = 16
    me = lax.axis_index("seq")
    load = pltpu.make_async_copy(cache_hbm, cache, cache_sem)
    load.start()

    barrier = pltpu.get_barrier_semaphore()
    for step in range(1, n):
        pl.semaphore_signal(barrier, inc=1, device_id={"seq": lax.rem(me + step, n)}, device_id_type=MESH)
    pl.semaphore_wait(barrier, n - 1)

    def exchange(buffer, send, recv):
        copies = [
            pltpu.make_async_remote_copy(
                src_ref=buffer.at[me],
                dst_ref=buffer.at[me],
                send_sem=send.at[step],
                recv_sem=recv.at[step],
                device_id={"seq": lax.rem(me + step, n)},
                device_id_type=MESH,
            )
            for step in range(1, n)
        ]
        for copy in copies:
            copy.start()
        for copy in copies:
            copy.wait()

    arrived[me] = dec_ref[...]
    exchange(arrived, send1, recv1)

    def gathered(part):
        return arrived[:, part].astype(F32).reshape(n * slots, local).astype(BF16)

    pick = pick_ref[...]
    q = rotate_columns(dot(gathered(0), pick, 0, 1).astype(BF16).astype(F32), cos_ref[...], sin_ref[...], 0.125).astype(F32)
    k = rotate_columns(dot(gathered(1), pick, 0, 1).astype(BF16).astype(F32), cos_ref[...], sin_ref[...], None).astype(F32)
    v = dot(pick, gathered(2), 1, 0).astype(BF16).astype(F32)
    load.wait()

    own_head = (
        lax.broadcasted_iota(jnp.int32, (local, rows), 0) // HEAD
        == lax.broadcasted_iota(jnp.int32, (local, rows), 1)
    )
    own_lane = (
        lax.broadcasted_iota(jnp.int32, (rows, local), 1) // HEAD
        == lax.broadcasted_iota(jnp.int32, (rows, local), 0)
    )
    attended = []
    for s in range(slots):
        query = jnp.where(own_head, q[:, s : s + 1], 0.0).astype(BF16)
        key = jnp.broadcast_to(k[:, s : s + 1], (local, 128)).astype(BF16)
        scores = dot(query, cache[s, 0], 0, 0) + bias_ref[s]
        own = dot(query, key, 0, 0)[:, :1]
        peak = jnp.maximum(jnp.max(scores, axis=-1, keepdims=True), own)
        exps = jnp.exp(scores - peak)
        own_exp = jnp.exp(own - peak)
        total = jnp.sum(exps, axis=-1, keepdims=True) + own_exp
        weights = (exps / total).astype(BF16)
        own_weight = (own_exp / total).astype(BF16).astype(F32)
        mixed = dot(weights, cache[s, 1], 1, 1) + own_weight * v[s : s + 1]
        attended.append(jnp.sum(jnp.where(own_lane, mixed, 0.0), axis=0, keepdims=True))
    results[me] = jnp.concatenate(attended, axis=0).astype(BF16)
    exchange(results, send2, recv2)
    every = results[...].astype(F32).reshape(n * slots, local).astype(BF16)
    out_ref[...] = dot(back_ref[...], every, 1, 0).astype(BF16)


def decode(n, dec, pick, back, cosine, sine, bias, cache):
    _, slots, local = dec.shape
    return pl.pallas_call(
        functools.partial(decode_kernel, n),
        in_specs=[VSPEC] * 6 + [ASPEC],
        out_specs=VSPEC,
        out_shape=jax.ShapeDtypeStruct((slots, local), BF16),
        scratch_shapes=[
            VMEM((n, 3, slots, local), BF16),
            VMEM((n, slots, local), BF16),
            VMEM(cache.shape, BF16),
            pltpu.SemaphoreType.DMA(()),
        ]
        + [pltpu.SemaphoreType.DMA((n,))] * 4,
        compiler_params=pltpu.CompilerParams(
            collective_id=0, has_side_effects=True, vmem_limit_bytes=32 * MIB
        ),
        name="decode",
    )(dec, pick, back, cosine, sine, bias, cache)


def prefill_kernel(chunk, q_ref, nk_ref, nv_ref, ck_ref, cv_ref, bias_ref, out_ref):
    rows = q_ref.shape[2]
    for start in range(0, rows, chunk):
        stop = start + chunk
        q = q_ref[0, :, start:stop]
        cached = dot(q, ck_ref[0], 0, 0) + bias_ref[...]
        causal = lax.broadcasted_iota(jnp.int32, (chunk, stop), 1) <= start + lax.broadcasted_iota(
            jnp.int32, (chunk, stop), 0
        )
        fresh = jnp.where(causal, dot(q, nk_ref[0, :, :stop], 0, 0), NEGATIVE)
        peak = jnp.maximum(
            jnp.max(cached, axis=-1, keepdims=True), jnp.max(fresh, axis=-1, keepdims=True)
        )
        cached = jnp.exp(cached - peak)
        fresh = jnp.exp(fresh - peak)
        scale = 1.0 / (
            jnp.sum(cached, axis=-1, keepdims=True) + jnp.sum(fresh, axis=-1, keepdims=True)
        )
        mixed = dot((cached * scale).astype(BF16), cv_ref[0], 1, 1)
        mixed += dot((fresh * scale).astype(BF16), nv_ref[0, :, :stop], 1, 1)
        out_ref[:, start:stop] = mixed.T.astype(BF16)


def prefill(projected, cache, bias):
    _, local, rows = projected.shape
    keys = cache.shape[2]
    head = lambda part, length: pl.BlockSpec((1, HEAD, length), lambda h: (part, h, 0))
    return pl.pallas_call(
        functools.partial(prefill_kernel, 256),
        grid=(local // HEAD,),
        in_specs=[
            head(0, rows), head(1, rows), head(2, rows), head(0, keys), head(1, keys),
            pl.BlockSpec((1, keys), lambda h: (0, 0)),
        ],
        out_specs=pl.BlockSpec((HEAD, rows), lambda h: (h, 0)),
        out_shape=jax.ShapeDtypeStruct((local, rows), BF16),
        compiler_params=pltpu.CompilerParams(vmem_limit_bytes=40 * MIB),
        name="prefill",
    )(projected, projected, projected, cache, cache, bias)


def output_kernel(
    att_ref, datt_ref, w_ref, tok_ref, dtok_ref, gain_ref,
    hid_ref, dhid_ref, nor_ref, dnor_ref,
    att, give, have, got1, pair, got2, done, got3, dec,
    s1, r1, s2, r2, s3, r3, sd, rd,
):
    rows = tok_ref.shape[0]
    half = rows // 2
    pieces, chunk = pair.shape[0], pair.shape[1]
    me = lax.axis_index("tp")
    side = lax.rem(me, 2)
    core = me + 1 - 2 * side
    across = lax.rem(me + 2, 4)
    mine = pl.multiple_of(side * half, half)
    other = pl.multiple_of((1 - side) * half, half)

    barrier = pltpu.get_barrier_semaphore()
    for step in range(1, 4):
        pl.semaphore_signal(barrier, inc=1, device_id={"tp": lax.rem(me + step, 4)}, device_id_type=MESH)
    pl.semaphore_wait(barrier, 3)

    def send(src, dst, ssem, rsem, to):
        return pltpu.make_async_remote_copy(
            src_ref=src, dst_ref=dst, send_sem=ssem, recv_sem=rsem,
            device_id={"tp": to}, device_id_type=MESH,
        )

    first = [send(give.at[j], got1.at[j], s1.at[j], r1.at[j], core) for j in range(pieces)]
    second = [send(pair.at[j], got2.at[j], s2.at[j], r2.at[j], across) for j in range(pieces)]
    third = [send(done.at[j], got3.at[j], s3.at[j], r3.at[j], core) for j in range(pieces)]
    small = [
        send(dec.at[me], dec.at[me], sd.at[step], rd.at[step], lax.rem(me + step, 4))
        for step in range(1, 4)
    ]

    att[...] = att_ref[...].astype(F32).T.astype(BF16)
    block = 2 * chunk
    for j in range(pieces // 2):
        part = jnp.dot(att[pl.ds(other + j * block, block), :], w_ref[...], preferred_element_type=F32)
        give[2 * j] = part[:chunk].astype(BF16)
        first[2 * j].start()
        give[2 * j + 1] = part[chunk:].astype(BF16)
        first[2 * j + 1].start()
    for j in range(pieces // 2):
        part = jnp.dot(att[pl.ds(mine + j * block, block), :], w_ref[...], preferred_element_type=F32)
        have[2 * j] = part[:chunk].astype(BF16)
        have[2 * j + 1] = part[chunk:].astype(BF16)
        for i in (2 * j, 2 * j + 1):
            first[i].wait_recv()
            pair[i] = (have[i].astype(F32) + got1[i].astype(F32)).astype(BF16)
            second[i].start()
    dec[me] = jnp.dot(datt_ref[...], w_ref[...], preferred_element_type=F32).astype(BF16)
    for copy in small:
        copy.start()
    for j in range(pieces):
        span = pl.ds(mine + j * chunk, chunk)
        second[j].wait_recv()
        combined = pair[j].astype(F32) + got2[j].astype(F32)
        hidden = (tok_ref[span, :].astype(F32) + combined).astype(BF16)
        done[j] = hidden
        third[j].start()
        hid_ref[span, :] = hidden
        nor_ref[span, :] = rms_rows(hidden.astype(F32), gain_ref[...])
        if j > 0:
            take(third[j - 1], got3, hid_ref, nor_ref, gain_ref, other, j - 1, chunk)
    take(third[pieces - 1], got3, hid_ref, nor_ref, gain_ref, other, pieces - 1, chunk)
    for copy in small:
        copy.wait_recv()
    total = dec[0].astype(F32) + dec[1].astype(F32) + dec[2].astype(F32) + dec[3].astype(F32)
    hidden = (dtok_ref[...].astype(F32) + total).astype(BF16)
    dhid_ref[...] = hidden
    dnor_ref[...] = rms_rows(hidden.astype(F32), gain_ref[...])
    for copy in first + second + third + small:
        copy.wait_send()


def take(copy, got, hid_ref, nor_ref, gain_ref, other, j, chunk):
    copy.wait_recv()
    span = pl.ds(other + j * chunk, chunk)
    hidden = got[j]
    hid_ref[span, :] = hidden
    nor_ref[span, :] = rms_rows(hidden.astype(F32), gain_ref[...])


def output(att, datt, w, tokens, decode_tokens, gain):
    rows, width = tokens.shape
    local = w.shape[0]
    drows = decode_tokens.shape[0]
    pieces = 4
    chunk = rows // 2 // pieces
    buffer = VMEM((pieces, chunk, width), BF16)
    sem = pltpu.SemaphoreType.DMA((pieces,))
    return pl.pallas_call(
        output_kernel,
        in_specs=[VSPEC] * 6,
        out_specs=[VSPEC] * 4,
        out_shape=[
            jax.ShapeDtypeStruct((rows, width), BF16),
            jax.ShapeDtypeStruct((drows, width), BF16),
            jax.ShapeDtypeStruct((rows, width), BF16),
            jax.ShapeDtypeStruct((drows, width), BF16),
        ],
        scratch_shapes=[VMEM((rows, local), BF16)]
        + [buffer] * 7
        + [VMEM((4, drows, width), BF16)]
        + [sem] * 6
        + [pltpu.SemaphoreType.DMA((4,))] * 2,
        compiler_params=pltpu.CompilerParams(
            collective_id=1, has_side_effects=True, vmem_limit_bytes=48 * MIB
        ),
        name="output",
    )(att, datt, w, tokens, decode_tokens, gain)


def local_step(
    n,
    prefill_tokens,
    decode_tokens,
    attention_gain,
    qkv_weight,
    out_weight,
    feedforward_gain,
    prefill_cache,
    prefill_offsets,
    decode_cache,
    decode_lengths,
    request_slot,
):
    rows, width = prefill_tokens.shape
    drows = decode_tokens.shape[0]
    exponent = jnp.arange(HALF, dtype=F32) * (2.0 / HEAD)
    frequency = (ROPE_BASE ** (-exponent))[:, None]
    positions = prefill_offsets[0].astype(F32) + jnp.arange(rows, dtype=F32)
    angles = frequency * positions[None, :]
    dangles = frequency * decode_lengths.astype(F32)[None, :]
    rank = lax.axis_index("seq")
    slots = jnp.arange(n * drows, dtype=jnp.int32)
    own = rank * drows + jnp.arange(drows, dtype=jnp.int32)
    pick = (request_slot[None, :] == own[:, None]).astype(BF16)
    my_slots = lax.dynamic_slice_in_dim(request_slot, rank * drows, drows)
    back = (my_slots[:, None] == slots[None, :]).astype(BF16)
    dmax = decode_cache.shape[2]
    dbias = jnp.where(
        jnp.arange(dmax, dtype=jnp.int32)[None, :] < decode_lengths[:, None], 0.0, NEGATIVE
    ).astype(F32)[:, None, :]
    pmax = prefill_cache.shape[2]
    pbias = jnp.where(jnp.arange(pmax, dtype=jnp.int32) < prefill_offsets[0], 0.0, NEGATIVE).astype(F32)[None, :]

    projected, dec = project(
        prefill_tokens, decode_tokens, attention_gain[None, :], qkv_weight.transpose(1, 2, 0),
        jnp.cos(angles), jnp.sin(angles),
    )
    datt = decode(
        n, dec, pick, back, jnp.cos(dangles), jnp.sin(dangles), dbias,
        decode_cache.transpose(0, 1, 3, 2),
    )
    att = prefill(projected, prefill_cache[0].transpose(0, 2, 1), pbias)
    hidden, dhidden, normed, dnormed = output(
        att, datt, out_weight, prefill_tokens, decode_tokens, feedforward_gain[None, :]
    )
    return hidden, dhidden, normed, dnormed


def solution(mesh):
    placed = (
        P("seq", None),
        P("seq", None),
        P(),
        P(None, None, "tp"),
        P("tp", None),
        P(),
        P("seq", None, None, "tp"),
        P("seq"),
        P("seq", None, None, "tp"),
        P("seq"),
        P(),
    )
    return jax.shard_map(
        functools.partial(local_step, mesh.shape["seq"]),
        mesh=mesh,
        in_specs=placed,
        out_specs=(P("seq", None), P("seq", None), P("seq", None), P("seq", None)),
        check_vma=False,
    )
```

time: 216 us -> 102 us (0.47)
  Pallas kernels: 0 us -> 85.7 us
  blocking collectives: 63.1 us -> 0 us
  waiting for transfers between devices: 57.6 us -> 0 us
  matrix products: 38.1 us -> 0 us
  other arithmetic: 22.4 us -> 2.59 us
  between operations: 15 us -> 1.38 us
  local copies, waits for them, and re-layouts: 19.3 us -> 11.9 us
    pallas_call x0 -> x4, Pallas kernels: none -> 85.7 us  [the longest x1 35.1 us: output(): pl.pallas_call(output_kernel, in_specs=[VSPEC] * 6, out_specs=[VSPEC] * 4...]
    all_gather x2 -> x0, blocking collectives: 63.1 us -> none  [the longest x1 32.5 us: local(): arrived = lax.all_gather(decode_block, 'seq', axis=0, tiled=True)]
    psum x1 -> x0, waiting for transfers between devices: 57.6 us -> none  [local(): lax.psum(partial_value.astype(jnp.bfloat16), 'tp').astype(jnp.float32)]
    dot_general x10 -> x0, matrix products: 38.1 us -> none  [the longest x1 8.62 us: local(): jnp.dot(normed_in, qkv_weight.reshape(model_width, 3 * local_width), pref...]
    slice x12 -> x0, local copies, waits for them, and re-layouts: 17.9 us -> none  [the longest x2 5.36 us: local(): prefill_block = projected[:span_rows]]
    reduce_sum x5 -> x0, other arithmetic: 16.1 us -> none  [the longest x2 5.77 us: rms_norm(): jnp.mean(widened * widened, axis=-1, keepdims=True) + RMS_EPSILON]
    unnamed x18 -> x16, local copies, waits for them, and re-layouts: 0.05 us -> 9.75 us
  transfers between devices with their start and end apart: 1 -> 0, of which waited for: 1 -> 0; matrix products, arithmetic and copies ran while one was open for 0% -> 0% of each run, Pallas kernels for 0% -> 0%
where the time goes in v1:
time: 102 us
  Pallas kernels  85.7 us (84%)
  local copies, waits for them, and re-layouts  11.9 us (12%)
  other arithmetic  2.59 us (3%)
  between operations  1.38 us (1%)
    pallas_call x1, Pallas kernels, output(): pl.pallas_call(output_kernel, in_specs=[VSPEC] * 6, out_specs=[VSPEC] * 4...  35.1 us
    pallas_call x1, Pallas kernels, decode(): pl.pallas_call(functools.partial(decode_kernel, n), in_specs=[VSPEC] * 6...  22.9 us
    pallas_call x1, Pallas kernels, prefill(): pl.pallas_call(functools.partial(prefill_kernel, 256), grid=(local // HEA...  18.9 us
    unnamed x16, local copies, waits for them, and re-layouts  9.75 us
    pallas_call x1, Pallas kernels, project(): pl.pallas_call(project_kernel, grid=(3,), in_specs=[whole((rows, width)),...  8.73 us

profile of v1, /device:TPU:0, one launch (start us, length us, event | category | flops | bytes accessed | tf_op | source)
XLA Modules:
  0.0 101.6 jit_solution(12560374450771885425)
XLA Ops:
  1.3 0.7 dynamic_slice.3
  2.0 0.7 convert_element_type.15
  2.7 0.7 fusion
  3.4 0.7 compare_select_fusion.bias_ref
  4.2 0.7 broadcast_in_dim.20.gain_ref
  4.9 0.7 broadcast_in_dim.38.gain_ref
  5.6 0.1 multiply_sine_fusion.1
  5.7 0.3 multiply_sine_fusion
  6.1 0.0 copy-start
  6.1 1.7 %copy-done = bf16[512,2304]{1,0:T(8,128)(2,1)S(1)} copy-done((bf16[512,2304]{1,0:T(8,128)(2,1)S(1)}, bf16[512,2304]{1,0:T(8,128)(2,1)}, u32[]{:S(2)}) %copy-start) | copy-done | bytes 2359320
  7.7 3.3 %copy-done.2 = bf16[2304,3,576]{0,2,1:T(8,128)(2,1)S(1)} copy-done((bf16[2304,3,576]{0,2,1:T(8,128)(2,1)S(1)}, bf16[2304,3,576]{0,2,1:T(8,128)(2,1)}, u32[]{:S(2)}) %copy-start.2) | copy-done | bytes 7962648
  11.0 0.8 copy-done.4
  11.8 8.7 %project.1 = (bf16[3,576,512]{2,1,0:T(8,128)(2,1)S(1)}, bf16[3,8,576]{2,1,0:T(8,128)(2,1)S(1)}) custom-call(bf16[512,2304]{1,0:T(8,128)(2,1)S(1)} %copy-done, bf16[8,2304]{1,0:T(8,128)(2,1)S(1)} %copy-done.4, f32[1,2304]{1,0:T(1,128)S(1)} %broadcast_in_dim.20.gain_ref, bf16[3,576,2304]{2,1,0:T(8,128)(2,1)S(1)} %bitcast.10, ...), custom_call_target="tpu_custom_call" | custom-call | tf_op jit(solution)/shard_map/project/pallas_call | solution.py:75
  20.5 0.0 copy-done.3
  20.5 0.0 copy-start.1
  20.5 22.9 %decode.1.datt_ref = bf16[8,576]{1,0:T(8,128)(2,1)S(1)} custom-call(bf16[3,8,576]{2,1,0:T(8,128)(2,1)S(1)} %get-tuple-element.7.dec_ref, bf16[8,64]{1,0:T(8,128)(2,1)S(1)} %get-tuple-element.13.pick_ref, bf16[8,64]{1,0:T(8,128)(2,1)S(1)} %get-tuple-element.12.back_ref, f32[32,8]{1,0:T(8,128)S(1)} %get-tuple-element.11.cos_ref, ...), custom_call_target="tpu_custom_call" | custom-call | tf_op jit(solution)/shard_map/decode/pallas_call | solution.py:176
  43.4 0.0 copy-done.1
  43.4 0.0 copy-start.5
  43.5 18.9 %prefill.1.att_ref = bf16[576,512]{1,0:T(8,128)(2,1)S(1)} custom-call(bf16[3,576,512]{2,1,0:T(8,128)(2,1)S(1)} %get-tuple-element.6.q_ref.nk_ref.nv_ref, bf16[3,576,512]{2,1,0:T(8,128)(2,1)S(1)} %get-tuple-element.6.q_ref.nk_ref.nv_ref, bf16[3,576,512]{2,1,0:T(8,128)(2,1)S(1)} %get-tuple-element.6.q_ref.nk_ref.nv_ref, bf16[2,576,1024]{2,1,0:T(8,128)(2,1)S(1)} %bitcast.8, ...), custom_call_target="tpu_custom_call" | custom-call | tf_op jit(solution)/shard_map/prefill/pallas_call | solution.py:222
  62.4 35.1 %output.1 = (bf16[512,2304]{1,0:T(8,128)(2,1)S(1)}, bf16[8,2304]{1,0:T(8,128)(2,1)S(1)}, bf16[512,2304]{1,0:T(8,128)(2,1)S(1)}, bf16[8,2304]{1,0:T(8,128)(2,1)S(1)}) custom-call(bf16[576,512]{1,0:T(8,128)(2,1)S(1)} %prefill.1.att_ref, bf16[8,576]{1,0:T(8,128)(2,1)S(1)} %decode.1.datt_ref, bf16[576,2304]{1,0:T(8,128)(2,1)} %w_ref.1, ...), custom_call_target="tpu_custom_call" | custom-call | tf_op jit(solution)/shard_map/output/pallas_call | solution.py:328
  97.5 1.4 %copy.21 = bf16[512,2304]{1,0:T(8,128)(2,1)} copy(bf16[512,2304]{1,0:T(8,128)(2,1)S(1)} %get-tuple-element.18) | data formatting | bytes 4718592
  98.9 0.6 copy.22
  99.5 1.4 %copy.23 = bf16[512,2304]{1,0:T(8,128)(2,1)} copy(bf16[512,2304]{1,0:T(8,128)(2,1)S(1)} %get-tuple-element.20) | data formatting | bytes 4718592
  100.9 0.6 copy.24
  (8 shorter events, 0.0 us)
Async XLA Ops:
  6.1 1.7 %copy-start = (bf16[512,2304]{1,0:T(8,128)(2,1)S(1)}, bf16[512,2304]{1,0:T(8,128)(2,1)}, u32[]{:S(2)}) copy-start(bf16[512,2304]{1,0:T(8,128)(2,1)} %tok_ref.3) | copy-start | bytes 7077892
  7.7 3.3 %copy-start.2 = (bf16[2304,3,576]{0,2,1:T(8,128)(2,1)S(1)}, bf16[2304,3,576]{0,2,1:T(8,128)(2,1)}, u32[]{:S(2)}) copy-start(bf16[2304,3,576]{0,2,1:T(8,128)(2,1)} %param.14) | copy-start | bytes 23887876
  11.0 0.8 copy-start.4
  11.8 8.7 %copy-start.3 = (bf16[8,2,256,576]{2,3,1,0:T(8,128)(2,1)S(1)}, bf16[8,2,256,576]{2,3,1,0:T(8,128)(2,1)}, u32[]{:S(2)}) copy-start(bf16[8,2,256,576]{2,3,1,0:T(8,128)(2,1)} %param.19) | copy-start | bytes 14155780
  20.5 22.9 %copy-start.1 = (bf16[1,2,1024,576]{2,3,1,0:T(8,128)(2,1)S(1)}, bf16[1,2,1024,576]{2,3,1,0:T(8,128)(2,1)}, u32[]{:S(2)}) copy-start(bf16[1,2,1024,576]{2,3,1,0:T(8,128)(2,1)} %param.17) | copy-start | bytes 7077892
  43.4 19.0 %copy-start.5 = (bf16[8,2304]{1,0:T(8,128)(2,1)S(1)}, bf16[8,2304]{1,0:T(8,128)(2,1)}, u32[]{:S(2)}) copy-start(bf16[8,2304]{1,0:T(8,128)(2,1)} %dtok_ref.3) | copy-start | bytes 110596

commit v2 on v0

v2 whole, which is shorter than its diff:
```python
import functools

import jax
import jax.numpy as jnp
from jax import lax
from jax.experimental import pallas as pl
from jax.experimental.pallas import tpu as pltpu
from jax.sharding import PartitionSpec as P

HEAD = 64
HALF = HEAD // 2
RMS_EPSILON = 1e-05
ROPE_BASE = 10000.0
NEGATIVE = -1e30
MIB = 1 << 20
F32, BF16 = jnp.float32, jnp.bfloat16
MESH = pl.DeviceIdType.MESH
VMEM = pltpu.VMEM
VSPEC = pl.BlockSpec(memory_space=pltpu.VMEM)
HSPEC = pl.BlockSpec(memory_space=pltpu.HBM)
SSPEC = pl.BlockSpec(memory_space=pltpu.SMEM)


def dot(a, b, ca, cb):
    return lax.dot_general(a, b, (((ca,), (cb,)), ((), ())), preferred_element_type=F32)


def rms_rows(x, gain):
    inverse = lax.rsqrt(jnp.mean(x * x, axis=-1, keepdims=True) + RMS_EPSILON)
    return (x * inverse * gain).astype(BF16)


def rotate_columns(x, cosine, sine, scale):
    pieces = []
    for head in range(x.shape[0] // HEAD):
        a = x[head * HEAD : head * HEAD + HALF]
        b = x[head * HEAD + HALF : (head + 1) * HEAD]
        pieces.append(a * cosine - b * sine)
        pieces.append(b * cosine + a * sine)
    turned = jnp.concatenate(pieces, axis=0).astype(BF16)
    return turned if scale is None else (turned.astype(F32) * scale).astype(BF16)


def project_kernel(
    gain_ref, cos_ref, sin_ref, tok_hbm, dtok_hbm, w_hbm, out_ref, dec_ref,
    tok, dtok, w, normed, dnormed, tok_sem, dtok_sem, w_sem,
):
    rows = tok.shape[0]
    loads = [pltpu.make_async_copy(w_hbm.at[part], w.at[part], w_sem.at[part]) for part in range(3)]
    tok_load = pltpu.make_async_copy(tok_hbm, tok, tok_sem)
    dtok_load = pltpu.make_async_copy(dtok_hbm, dtok, dtok_sem)
    tok_load.start()
    dtok_load.start()
    for load in loads:
        load.start()
    gain = gain_ref[...].reshape(1, gain_ref.shape[0])
    tok_load.wait()

    @pl.loop(0, rows // 64)
    def _(i):
        span = pl.ds(pl.multiple_of(i * 64, 64), 64)
        normed[span, :] = rms_rows(tok[span, :].astype(F32), gain)

    dtok_load.wait()
    dnormed[...] = rms_rows(dtok[...].astype(F32), gain)
    for part in range(3):
        loads[part].wait()
        product = dot(w[part], normed[...], 1, 1).astype(BF16)
        dec_ref[part] = dot(dnormed[...], w[part], 1, 1).astype(BF16)
        if part < 2:
            product = rotate_columns(
                product.astype(F32), cos_ref[:, :rows], sin_ref[:, :rows], 0.125 if part == 0 else None
            )
        out_ref[part] = product


def project(tokens, decode_tokens, gain, w, cosine, sine):
    rows, width = tokens.shape
    drows = decode_tokens.shape[0]
    local = w.shape[1]
    return pl.pallas_call(
        project_kernel,
        in_specs=[VSPEC] * 3 + [HSPEC] * 3,
        out_specs=[VSPEC] * 2,
        out_shape=[
            jax.ShapeDtypeStruct((3, local, rows), BF16),
            jax.ShapeDtypeStruct((3, drows, local), BF16),
        ],
        scratch_shapes=[
            VMEM((rows, width), BF16),
            VMEM((drows, width), BF16),
            VMEM((3, local, width), BF16),
            VMEM((rows, width), BF16),
            VMEM((drows, width), BF16),
            pltpu.SemaphoreType.DMA(()),
            pltpu.SemaphoreType.DMA(()),
            pltpu.SemaphoreType.DMA((3,)),
        ],
        compiler_params=pltpu.CompilerParams(vmem_limit_bytes=48 * MIB),
        name="project",
    )(gain, cosine, sine, tokens, decode_tokens, w)


def attention_kernel(
    n, proj_ref, dec_ref, cos_ref, sin_ref, slot_ref, offset_ref, length_ref,
    pcache_hbm, dcache_hbm, w_hbm, tok_hbm, dtok_hbm,
    hid_ref, dhid_ref,
    arrived, results, routed, pcache, dcache, w, tok, dtok, att, part, got1, pair, got2, dec,
    load_sem, send1, recv1, send2, recv2, s1, r1, s2, r2, s3, r3, sd, rd,
):
    slots, local = dec_ref.shape[1:]
    heads = local // HEAD
    rows = tok.shape[0]
    pieces, chunk = part.shape[:2]
    own_rows = chunk // 2
    keys = pcache.shape[2]
    dkeys = dcache.shape[3]
    seq = lax.axis_index("seq")
    tp = lax.axis_index("tp")
    side = lax.rem(tp, 2)
    core = tp + 1 - 2 * side
    across = lax.rem(tp + 2, 4)
    mine = pl.multiple_of(side * own_rows, own_rows)
    other = pl.multiple_of((1 - side) * own_rows, own_rows)

    loads = [
        pltpu.make_async_copy(src, dst, load_sem.at[i])
        for i, (src, dst) in enumerate(
            ((pcache_hbm, pcache), (w_hbm, w), (dcache_hbm, dcache), (tok_hbm, tok), (dtok_hbm, dtok))
        )
    ]
    for load in loads:
        load.start()

    barrier = pltpu.get_barrier_semaphore()
    for step in range(1, n):
        pl.semaphore_signal(barrier, inc=1, device_id={"seq": lax.rem(seq + step, n)}, device_id_type=MESH)
    for step in range(1, 4):
        pl.semaphore_signal(barrier, inc=1, device_id={"tp": lax.rem(tp + step, 4)}, device_id_type=MESH)
    pl.semaphore_wait(barrier, n + 2)

    def spread(buffer, send, recv):
        return [
            pltpu.make_async_remote_copy(
                src_ref=buffer.at[seq],
                dst_ref=buffer.at[seq],
                send_sem=send.at[step],
                recv_sem=recv.at[step],
                device_id={"seq": lax.rem(seq + step, n)},
                device_id_type=MESH,
            )
            for step in range(1, n)
        ]

    def send(src, dst, ssem, rsem, to):
        return pltpu.make_async_remote_copy(
            src_ref=src, dst_ref=dst, send_sem=ssem, recv_sem=rsem,
            device_id={"tp": to}, device_id_type=MESH,
        )

    def owned(c):
        return pl.ds(c * chunk + mine, own_rows)

    there = spread(arrived, send1, recv1)
    back = spread(results, send2, recv2)
    first = [
        send(part.at[c, pl.ds(other, own_rows)], got1.at[c], s1.at[c], r1.at[c], core) for c in range(pieces)
    ]
    second = [send(pair.at[c], got2.at[c], s2.at[c], r2.at[c], across) for c in range(pieces)]
    third = [send(hid_ref.at[owned(c)], hid_ref.at[owned(c)], s3.at[c], r3.at[c], core) for c in range(pieces)]
    small = [
        send(dec.at[tp], dec.at[tp], sd.at[step], rd.at[step], lax.rem(tp + step, 4)) for step in range(1, 4)
    ]

    arrived[seq] = dec_ref[...]
    for copy in there:
        copy.start()

    def cross(c):
        first[c].wait_recv()
        pair[c] = (part[c, pl.ds(mine, own_rows)].astype(F32) + got1[c].astype(F32)).astype(BF16)
        second[c].start()

    loads[0].wait()
    bias = jnp.where(lax.broadcasted_iota(jnp.int32, (1, keys), 1) < offset_ref[0], 0.0, NEGATIVE)
    for c in range(pieces):
        start, stop = c * chunk, (c + 1) * chunk

        @pl.loop(0, heads // 3)
        def _(group):
            for i in range(3):
                head = pl.ds(pl.multiple_of(group * (3 * HEAD) + i * HEAD, HEAD), HEAD)
                q = proj_ref[0, head, start:stop]
                cached = dot(q, pcache[0, head, :], 0, 0) + bias
                causal = lax.broadcasted_iota(jnp.int32, (chunk, stop), 1) <= start + lax.broadcasted_iota(
                    jnp.int32, (chunk, stop), 0
                )
                fresh = jnp.where(causal, dot(q, proj_ref[1, head, :stop], 0, 0), NEGATIVE)
                peak = jnp.maximum(
                    jnp.max(cached, axis=-1, keepdims=True), jnp.max(fresh, axis=-1, keepdims=True)
                )
                cached = jnp.exp(cached - peak)
                fresh = jnp.exp(fresh - peak)
                scale = 1.0 / (
                    jnp.sum(cached, axis=-1, keepdims=True) + jnp.sum(fresh, axis=-1, keepdims=True)
                )
                mixed = dot((cached * scale).astype(BF16), pcache[1, head, :], 1, 1)
                mixed += dot((fresh * scale).astype(BF16), proj_ref[2, head, :stop], 1, 1)
                att[head, :] = mixed.T.astype(BF16)
            if c > 0:

                @pl.when(group == 0)
                def _():
                    cross(c - 1)

        if c == 0:
            loads[1].wait()
        part[c] = dot(att[...], w[...], 0, 0).astype(BF16)
        first[c].start()

    for copy in there:
        copy.wait()
    cross(pieces - 1)
    loads[3].wait()

    def finish(c):
        second[c].wait_recv()
        combined = pair[c].astype(F32) + got2[c].astype(F32)
        hid_ref[owned(c), :] = (tok[owned(c), :].astype(F32) + combined).astype(BF16)
        third[c].start()

    total = n * slots
    chosen = seq * slots + lax.broadcasted_iota(jnp.int32, (slots, total), 0)
    slot_row = slot_ref[...].reshape(1, total)
    pick = (slot_row == chosen).astype(F32).astype(BF16)
    placing = (slot_row == lax.broadcasted_iota(jnp.int32, (total, total), 0)).astype(F32).astype(BF16)

    def gathered(which):
        return arrived[:, which].astype(F32).reshape(total, local).astype(BF16)

    dcos, dsin = cos_ref[:, rows:], sin_ref[:, rows:]
    q = rotate_columns(dot(gathered(0), pick, 0, 1).astype(BF16).astype(F32), dcos, dsin, 0.125).astype(F32)
    k = rotate_columns(dot(gathered(1), pick, 0, 1).astype(BF16).astype(F32), dcos, dsin, None).astype(F32)
    v = dot(pick, gathered(2), 1, 0).astype(BF16).astype(F32)
    padded = 16
    own_head = (
        lax.broadcasted_iota(jnp.int32, (local, padded), 0) // HEAD
        == lax.broadcasted_iota(jnp.int32, (local, padded), 1)
    )
    own_lane = (
        lax.broadcasted_iota(jnp.int32, (padded, local), 1) // HEAD
        == lax.broadcasted_iota(jnp.int32, (padded, local), 0)
    )
    loads[2].wait()
    position = lax.broadcasted_iota(jnp.int32, (1, dkeys), 1)
    attended = []
    for s in range(slots):
        query = jnp.where(own_head, q[:, s : s + 1], 0.0).astype(BF16)
        key = jnp.broadcast_to(k[:, s : s + 1], (local, 128)).astype(BF16)
        scores = dot(query, dcache[s, 0], 0, 0) + jnp.where(position < length_ref[s], 0.0, NEGATIVE)
        own = dot(query, key, 0, 0)[:, :1]
        peak = jnp.maximum(jnp.max(scores, axis=-1, keepdims=True), own)
        exps = jnp.exp(scores - peak)
        own_exp = jnp.exp(own - peak)
        denominator = jnp.sum(exps, axis=-1, keepdims=True) + own_exp
        weights = (exps / denominator).astype(BF16)
        own_weight = (own_exp / denominator).astype(BF16).astype(F32)
        mixed = dot(weights, dcache[s, 1], 1, 1) + own_weight * v[s : s + 1]
        attended.append(jnp.sum(jnp.where(own_lane, mixed, 0.0), axis=0, keepdims=True))
    results[seq] = jnp.concatenate(attended, axis=0).astype(BF16)
    for copy in back:
        copy.start()
    for c in range(pieces - 1):
        finish(c)
    for copy in back:
        copy.wait()
    every = results[...].astype(F32).reshape(total, local).astype(BF16)
    routed[...] = dot(placing, every, 0, 0)
    returned = routed[pl.ds(pl.multiple_of(seq * slots, slots), slots), :].astype(BF16)
    dec[tp] = dot(returned, w[...], 1, 0).astype(BF16)
    for copy in small:
        copy.start()
    finish(pieces - 1)
    for copy in small:
        copy.wait_recv()
    loads[4].wait()
    combined = dec[0].astype(F32) + dec[1].astype(F32) + dec[2].astype(F32) + dec[3].astype(F32)
    dhid_ref[...] = (dtok[...].astype(F32) + combined).astype(BF16)
    for copy in third:
        copy.wait_recv()
    for copy in first + second + third + small:
        copy.wait_send()


def attention(n, projected, dec, cosine, sine, slot, offset, lengths, pcache, dcache, w, tokens, decode_tokens):
    rows, width = tokens.shape
    _, slots, local = dec.shape
    pieces = 4
    chunk = rows // pieces
    buffer = VMEM((pieces, chunk // 2, width), BF16)
    sem = pltpu.SemaphoreType.DMA((pieces,))
    return pl.pallas_call(
        functools.partial(attention_kernel, n),
        in_specs=[VSPEC] * 5 + [SSPEC] * 2 + [HSPEC] * 5,
        out_specs=[VSPEC] * 2,
        out_shape=[jax.ShapeDtypeStruct((rows, width), BF16), jax.ShapeDtypeStruct((slots, width), BF16)],
        scratch_shapes=[
            VMEM((n, 3, slots, local), BF16),
            VMEM((n, slots, local), BF16),
            VMEM((n * slots, local), F32),
            VMEM(pcache.shape, BF16),
            VMEM(dcache.shape, BF16),
            VMEM(w.shape, BF16),
            VMEM((rows, width), BF16),
            VMEM((slots, width), BF16),
            VMEM((local, chunk), BF16),
            VMEM((pieces, chunk, width), BF16),
            buffer, buffer, buffer,
            VMEM((4, slots, width), BF16),
            pltpu.SemaphoreType.DMA((5,)),
        ]
        + [pltpu.SemaphoreType.DMA((n,))] * 4
        + [sem] * 6
        + [pltpu.SemaphoreType.DMA((4,))] * 2,
        compiler_params=pltpu.CompilerParams(
            collective_id=0, has_side_effects=True, vmem_limit_bytes=48 * MIB
        ),
        name="attention",
    )(projected, dec, cosine, sine, slot, offset, lengths, pcache, dcache, w, tokens, decode_tokens)


def norm_kernel(gain_ref, in_ref, din_ref, hid_ref, dhid_ref, nor_ref, dnor_ref):
    gain = gain_ref[...].reshape(1, gain_ref.shape[0])
    hidden = in_ref[...]
    hid_ref[...] = hidden
    nor_ref[...] = rms_rows(hidden.astype(F32), gain)

    @pl.when(pl.program_id(0) == 0)
    def _():
        dhidden = din_ref[...]
        dhid_ref[...] = dhidden
        dnor_ref[...] = rms_rows(dhidden.astype(F32), gain)


def final_norm(gain, hidden, dhidden):
    rows, width = hidden.shape
    block = 128
    tile = pl.BlockSpec((block, width), lambda i: (i, 0))
    small = pl.BlockSpec(dhidden.shape, lambda i: (0, 0))
    return pl.pallas_call(
        norm_kernel,
        grid=(rows // block,),
        in_specs=[pl.BlockSpec((width,), lambda i: (0,)), tile, small],
        out_specs=[tile, small, tile, small],
        out_shape=[jax.ShapeDtypeStruct(x.shape, BF16) for x in (hidden, dhidden, hidden, dhidden)],
        compiler_params=pltpu.CompilerParams(vmem_limit_bytes=32 * MIB),
        name="final_norm",
    )(gain, hidden, dhidden)


def local_step(
    n,
    prefill_tokens,
    decode_tokens,
    attention_gain,
    qkv_weight,
    out_weight,
    feedforward_gain,
    prefill_cache,
    prefill_offsets,
    decode_cache,
    decode_lengths,
    request_slot,
):
    rows = prefill_tokens.shape[0]
    exponent = jnp.arange(HALF, dtype=F32) * (2.0 / HEAD)
    frequency = (ROPE_BASE ** (-exponent))[:, None]
    positions = jnp.concatenate(
        [prefill_offsets[0].astype(F32) + jnp.arange(rows, dtype=F32), decode_lengths.astype(F32)]
    )
    angles = frequency * positions[None, :]
    cosine, sine = jnp.cos(angles), jnp.sin(angles)
    projected, dec = project(
        prefill_tokens, decode_tokens, attention_gain, qkv_weight.transpose(1, 2, 0), cosine, sine
    )
    hidden, dhidden = attention(
        n, projected, dec, cosine, sine, request_slot, prefill_offsets, decode_lengths,
        prefill_cache[0].transpose(0, 2, 1), decode_cache.transpose(0, 1, 3, 2), out_weight,
        prefill_tokens, decode_tokens,
    )
    hidden, dhidden, normed, dnormed = final_norm(feedforward_gain, hidden, dhidden)
    return hidden, dhidden, normed, dnormed


def solution(mesh):
    placed = (
        P("seq", None),
        P("seq", None),
        P(),
        P(None, None, "tp"),
        P("tp", None),
        P(),
        P("seq", None, None, "tp"),
        P("seq"),
        P("seq", None, None, "tp"),
        P("seq"),
        P(),
    )
    return jax.shard_map(
        functools.partial(local_step, mesh.shape["seq"]),
        mesh=mesh,
        in_specs=placed,
        out_specs=(P("seq", None), P("seq", None), P("seq", None), P("seq", None)),
        check_vma=False,
    )
```

time: 216 us -> 63.1 us (0.29)
  blocking collectives: 63.1 us -> 0 us
  waiting for transfers between devices: 57.6 us -> 0 us
  Pallas kernels: 0 us -> 57.2 us
  matrix products: 38.1 us -> 0 us
  other arithmetic: 22.4 us -> 1.05 us
  local copies, waits for them, and re-layouts: 19.3 us -> 3.15 us
  between operations: 15 us -> 1.35 us
    all_gather x2 -> x0, blocking collectives: 63.1 us -> none  [the longest x1 32.5 us: local(): arrived = lax.all_gather(decode_block, 'seq', axis=0, tiled=True)]
    psum x1 -> x0, waiting for transfers between devices: 57.6 us -> none  [local(): lax.psum(partial_value.astype(jnp.bfloat16), 'tp').astype(jnp.float32)]
    pallas_call x0 -> x3, Pallas kernels: none -> 57.2 us  [the longest x1 45.3 us: attention(): pl.pallas_call(functools.partial(attention_kernel, n), in_specs=[VSPEC] *...]
    dot_general x10 -> x0, matrix products: 38.1 us -> none  [the longest x1 8.62 us: local(): jnp.dot(normed_in, qkv_weight.reshape(model_width, 3 * local_width), pref...]
    slice x12 -> x0, local copies, waits for them, and re-layouts: 17.9 us -> none  [the longest x2 5.36 us: local(): prefill_block = projected[:span_rows]]
    reduce_sum x5 -> x0, other arithmetic: 16.1 us -> none  [the longest x2 5.77 us: rms_norm(): jnp.mean(widened * widened, axis=-1, keepdims=True) + RMS_EPSILON]
    unnamed x18 -> x12, local copies, waits for them, and re-layouts: 0.05 us -> 3.15 us
    convert_element_type x8 -> x1, other arithmetic: 2.94 us -> 0.66 us  [local_step(): decode_lengths.astype(F32)]
  transfers between devices with their start and end apart: 1 -> 0, of which waited for: 1 -> 0; matrix products, arithmetic and copies ran while one was open for 0% -> 0% of each run, Pallas kernels for 0% -> 0%
where the time goes in v2:
time: 63.1 us; the launch traced here: 62.8 us
  Pallas kernels  57.2 us (91%)
  local copies, waits for them, and re-layouts  3.15 us (5%)
  between operations  1.35 us (2%)
  other arithmetic  1.05 us (2%)
    pallas_call x1, Pallas kernels, attention(): pl.pallas_call(functools.partial(attention_kernel, n), in_specs=[VSPEC] *...  45.3 us
    pallas_call x1, Pallas kernels, project(): pl.pallas_call(project_kernel, in_specs=[VSPEC] * 3 + [HSPEC] * 3, out_sp...  8.74 us
    pallas_call x1, Pallas kernels, final_norm(): pl.pallas_call(norm_kernel, grid=(rows // block,), in_specs=[pl.BlockSpec...  3.22 us
    unnamed x12, local copies, waits for them, and re-layouts  3.15 us

profile of v2, /device:TPU:0, one launch (start us, length us, event | category | flops | bytes accessed | tf_op | source)
XLA Modules:
  0.0 62.8 jit_solution(15046463675415540839)
XLA Ops:
  1.3 0.7 %convert_element_type.11 = f32[8]{0:T(128)S(1)} convert(s32[8]{0:T(128)} %length_ref.1) | non-fusion elementwise | flops 8 | bytes 64 | tf_op jit(solution)/shard_map/convert_element_type | solution.py:379
  2.0 0.4 multiply_sine_fusion
  2.3 0.0 copy-start
  2.4 1.7 %copy-done = bf16[512,2304]{1,0:T(8,128)(2,1)S(1)} copy-done((bf16[512,2304]{1,0:T(8,128)(2,1)S(1)}, bf16[512,2304]{1,0:T(8,128)(2,1)}, u32[]{:S(2)}) %copy-start) | copy-done | bytes 2359320
  4.0 0.0 copy-start.1
  4.0 0.8 %copy-done.1 = bf16[8,2304]{1,0:T(8,128)(2,1)S(1)} copy-done((bf16[8,2304]{1,0:T(8,128)(2,1)S(1)}, bf16[8,2304]{1,0:T(8,128)(2,1)}, u32[]{:S(2)}) %copy-start.1) | copy-done | bytes 36888
  4.8 0.0 copy-start.2
  4.8 0.7 %copy-done.2 = f32[2304]{0:T(1024)S(1)} copy-done((f32[2304]{0:T(1024)S(1)}, f32[2304]{0:T(1024)}, u32[]{:S(2)}) %copy-start.2) | copy-done | bytes 9240
  5.5 0.0 copy-start.4
  5.5 0.0 copy-start.5
  5.5 8.7 %project.1 = (bf16[3,576,512]{2,1,0:T(8,128)(2,1)S(1)}, bf16[3,8,576]{2,1,0:T(8,128)(2,1)S(1)}) custom-call(f32[2304]{0:T(1024)S(1)} %copy-done.2, f32[32,520]{1,0:T(8,128)S(1)} %get-tuple-element.13.cos_ref, f32[32,520]{1,0:T(8,128)S(1)} %get-tuple-element.12.sin_ref, bf16[512,2304]{1,0:T(8,128)(2,1)S(1)} %copy-done, bf16[8,2304]{1,0:T(8,128)(2,1)S(1)} %copy-done.1, ...), custom_call_target="tpu_custom_call" | custom-call | tf_op jit(solution)/shard_map/project/pallas_call | solution.py:81
  14.2 0.0 copy-done.4
  14.2 0.0 copy-done.5
  14.3 0.0 copy-start.3
  14.3 45.3 %attention.1 = (bf16[512,2304]{1,0:T(8,128)(2,1)S(1)}, bf16[8,2304]{1,0:T(8,128)(2,1)S(1)}) custom-call(bf16[3,576,512]{2,1,0:T(8,128)(2,1)S(1)} %get-tuple-element.8.proj_ref, bf16[3,8,576]{2,1,0:T(8,128)(2,1)S(1)} %get-tuple-element.9.dec_ref, f32[32,520]{1,0:T(8,128)S(1)} %get-tuple-element.13.cos_ref, f32[32,520]{1,0:T(8,128)S(1)} %get-tuple-element.12.sin_ref, ...), custom_call_target="tpu_custom_call" | custom-call | tf_op jit(solution)/shard_map/attention/pallas_call | solution.py:302
  59.5 0.0 copy-done.3
  59.6 3.2 %final_norm.1 = (bf16[512,2304]{1,0:T(8,128)(2,1)}, bf16[8,2304]{1,0:T(8,128)(2,1)}, bf16[512,2304]{1,0:T(8,128)(2,1)}, bf16[8,2304]{1,0:T(8,128)(2,1)}) custom-call(f32[2304]{0:T(1024)S(1)} %copy-done.3, bf16[512,2304]{1,0:T(8,128)(2,1)S(1)} %get-tuple-element.10.in_ref, bf16[8,2304]{1,0:T(8,128)(2,1)S(1)} %get-tuple-element.11.din_ref), custom_call_target="tpu_custom_call" | custom-call | tf_op jit(solution)/shard_map/final_norm/pallas_call | solution.py:350
  (3 shorter events, 0.0 us)
Async XLA Ops:
  2.3 1.7 %copy-start = (bf16[512,2304]{1,0:T(8,128)(2,1)S(1)}, bf16[512,2304]{1,0:T(8,128)(2,1)}, u32[]{:S(2)}) copy-start(bf16[512,2304]{1,0:T(8,128)(2,1)} %tok_hbm.3) | copy-start | bytes 7077892
  4.0 0.8 %copy-start.1 = (bf16[8,2304]{1,0:T(8,128)(2,1)S(1)}, bf16[8,2304]{1,0:T(8,128)(2,1)}, u32[]{:S(2)}) copy-start(bf16[8,2304]{1,0:T(8,128)(2,1)} %dtok_hbm.3) | copy-start | bytes 110596
  4.8 0.7 %copy-start.2 = (f32[2304]{0:T(1024)S(1)}, f32[2304]{0:T(1024)}, u32[]{:S(2)}) copy-start(f32[2304]{0:T(1024)} %gain_ref.2) | copy-start | bytes 27652
  5.5 8.8 %copy-start.4 = (s32[8]{0:T(128)S(1)}, s32[8]{0:T(128)}, u32[]{:S(2)}) copy-start(s32[8]{0:T(128)} %length_ref.1) | copy-start | bytes 100
  5.5 8.8 %copy-start.5 = (s32[64]{0:T(128)S(1)}, s32[64]{0:T(128)}, u32[]{:S(2)}) copy-start(s32[64]{0:T(128)} %slot_ref.1) | copy-start | bytes 772
  14.3 45.3 %copy-start.3 = (f32[2304]{0:T(1024)S(1)}, f32[2304]{0:T(1024)}, u32[]{:S(2)}) copy-start(f32[2304]{0:T(1024)} %gain_ref.3) | copy-start | bytes 27652

commit v3 on v2

--- a/solution.py
+++ b/solution.py
@@ -96,19 +96,19 @@
             pltpu.SemaphoreType.DMA(()),
             pltpu.SemaphoreType.DMA((3,)),
         ],
-        compiler_params=pltpu.CompilerParams(vmem_limit_bytes=48 * MIB),
+        compiler_params=pltpu.CompilerParams(vmem_limit_bytes=59 * MIB),
         name="project",
     )(gain, cosine, sine, tokens, decode_tokens, w)
 
 
 def attention_kernel(
-    n, proj_ref, dec_ref, cos_ref, sin_ref, slot_ref, offset_ref, length_ref,
+    n, proj_hbm, dec_hbm, cos_ref, sin_ref, slot_ref, offset_ref, length_ref,
     pcache_hbm, dcache_hbm, w_hbm, tok_hbm, dtok_hbm,
     hid_ref, dhid_ref,
-    arrived, results, routed, pcache, dcache, w, tok, dtok, att, part, got1, pair, got2, dec,
+    arrived, results, routed, proj_ref, pcache, dcache, w, tok, dtok, att, part, got1, pair, got2, dec,
     load_sem, send1, recv1, send2, recv2, s1, r1, s2, r2, s3, r3, sd, rd,
 ):
-    slots, local = dec_ref.shape[1:]
+    slots, local = arrived.shape[2:]
     heads = local // HEAD
     rows = tok.shape[0]
     pieces, chunk = part.shape[:2]
@@ -129,6 +129,10 @@
             ((pcache_hbm, pcache), (w_hbm, w), (dcache_hbm, dcache), (tok_hbm, tok), (dtok_hbm, dtok))
         )
     ]
+    dec_load = pltpu.make_async_copy(dec_hbm, arrived.at[seq], load_sem.at[5])
+    proj_load = pltpu.make_async_copy(proj_hbm, proj_ref, load_sem.at[6])
+    dec_load.start()
+    proj_load.start()
     for load in loads:
         load.start()
 
@@ -172,7 +176,7 @@
         send(dec.at[tp], dec.at[tp], sd.at[step], rd.at[step], lax.rem(tp + step, 4)) for step in range(1, 4)
     ]
 
-    arrived[seq] = dec_ref[...]
+    dec_load.wait()
     for copy in there:
         copy.start()
 
@@ -181,6 +185,7 @@
         pair[c] = (part[c, pl.ds(mine, own_rows)].astype(F32) + got1[c].astype(F32)).astype(BF16)
         second[c].start()
 
+    proj_load.wait()
     loads[0].wait()
     bias = jnp.where(lax.broadcasted_iota(jnp.int32, (1, keys), 1) < offset_ref[0], 0.0, NEGATIVE)
     for c in range(pieces):
@@ -253,19 +258,33 @@
     )
     loads[2].wait()
     position = lax.broadcasted_iota(jnp.int32, (1, dkeys), 1)
+    product = q * k
+    own = jnp.concatenate(
+        [
+            jnp.sum(product[head * HEAD : (head + 1) * HEAD], axis=0, keepdims=True)
+            if head < heads
+            else jnp.zeros((1, slots), F32)
+            for head in range(padded)
+        ],
+        axis=0,
+    )
+    own = jnp.concatenate([own[:, s : s + 1] for s in range(slots)], axis=0)
+    scores = []
+    for s in range(slots):
+        query = jnp.where(own_head, q[:, s : s + 1], 0.0).astype(BF16)
+        hidden_keys = jnp.where(position < length_ref[s], 0.0, NEGATIVE)
+        scores.append(dot(query, dcache[s, 0], 0, 0) + hidden_keys)
+    scores = jnp.concatenate(scores, axis=0)
+    peak = jnp.maximum(jnp.max(scores, axis=-1, keepdims=True), own)
+    exps = jnp.exp(scores - peak)
+    own_exp = jnp.exp(own - peak)
+    denominator = jnp.sum(exps, axis=-1, keepdims=True) + own_exp
+    weights = (exps / denominator).astype(BF16)
+    own_weight = (own_exp / denominator).astype(BF16).astype(F32)
     attended = []
     for s in range(slots):
-        query = jnp.where(own_head, q[:, s : s + 1], 0.0).astype(BF16)
-        key = jnp.broadcast_to(k[:, s : s + 1], (local, 128)).astype(BF16)
-        scores = dot(query, dcache[s, 0], 0, 0) + jnp.where(position < length_ref[s], 0.0, NEGATIVE)
-        own = dot(query, key, 0, 0)[:, :1]
-        peak = jnp.maximum(jnp.max(scores, axis=-1, keepdims=True), own)
-        exps = jnp.exp(scores - peak)
-        own_exp = jnp.exp(own - peak)
-        denominator = jnp.sum(exps, axis=-1, keepdims=True) + own_exp
-        weights = (exps / denominator).astype(BF16)
-        own_weight = (own_exp / denominator).astype(BF16).astype(F32)
-        mixed = dot(weights, dcache[s, 1], 1, 1) + own_weight * v[s : s + 1]
+        span = slice(s * padded, (s + 1) * padded)
+        mixed = dot(weights[span], dcache[s, 1], 1, 1) + own_weight[span] * v[s : s + 1]
         attended.append(jnp.sum(jnp.where(own_lane, mixed, 0.0), axis=0, keepdims=True))
     results[seq] = jnp.concatenate(attended, axis=0).astype(BF16)
     for copy in back:
@@ -301,13 +320,14 @@
     sem = pltpu.SemaphoreType.DMA((pieces,))
     return pl.pallas_call(
         functools.partial(attention_kernel, n),
-        in_specs=[VSPEC] * 5 + [SSPEC] * 2 + [HSPEC] * 5,
+        in_specs=[HSPEC] * 2 + [VSPEC] * 3 + [SSPEC] * 2 + [HSPEC] * 5,
         out_specs=[VSPEC] * 2,
         out_shape=[jax.ShapeDtypeStruct((rows, width), BF16), jax.ShapeDtypeStruct((slots, width), BF16)],
         scratch_shapes=[
             VMEM((n, 3, slots, local), BF16),
             VMEM((n, slots, local), BF16),
             VMEM((n * slots, local), F32),
+            VMEM(projected.shape, BF16),
             VMEM(pcache.shape, BF16),
             VMEM(dcache.shape, BF16),
             VMEM(w.shape, BF16),
@@ -317,7 +337,7 @@
             VMEM((pieces, chunk, width), BF16),
             buffer, buffer, buffer,
             VMEM((4, slots, width), BF16),
-            pltpu.SemaphoreType.DMA((5,)),
+            pltpu.SemaphoreType.DMA((7,)),
         ]
         + [pltpu.SemaphoreType.DMA((n,))] * 4
         + [sem] * 6

time: 63.1 us -> 66.6 us (1.055)
  Pallas kernels: 57.2 us -> 61 us
  local copies, waits for them, and re-layouts: 3.15 us -> 2.25 us
  other arithmetic: 1.05 us -> 1.72 us
    pallas_call x1, Pallas kernels: 8.74 us -> 13.1 us  [project(): pl.pallas_call(project_kernel, in_specs=[VSPEC] * 3 + [HSPEC] * 3, out_sp...]
    unnamed x12 -> x16, local copies, waits for them, and re-layouts: 3.15 us -> 2.25 us
    sin x1, other arithmetic: 0.36 us -> 1.03 us  [local_step(): cosine, sine = (jnp.cos(angles), jnp.sin(angles))]
where the time goes in v3:
time: 66.6 us; the launch traced here: 66.3 us
  Pallas kernels  61 us (92%)
  local copies, waits for them, and re-layouts  2.25 us (3%)
  other arithmetic  1.72 us (3%)
  between operations  1.37 us (2%)
    pallas_call x1, Pallas kernels, attention(): pl.pallas_call(functools.partial(attention_kernel, n), in_specs=[HSPEC] *...  44.6 us
    pallas_call x1, Pallas kernels, project(): pl.pallas_call(project_kernel, in_specs=[VSPEC] * 3 + [HSPEC] * 3, out_sp...  13.1 us
    pallas_call x1, Pallas kernels, final_norm(): pl.pallas_call(norm_kernel, grid=(rows // block,), in_specs=[pl.BlockSpec...  3.23 us
    unnamed x16, local copies, waits for them, and re-layouts  2.25 us

profile of v3, /device:TPU:0, one launch (start us, length us, event | category | flops | bytes accessed | tf_op | source)
XLA Modules:
  0.0 66.3 jit_solution(3888139203736146981)
XLA Ops:
  1.3 0.7 convert_element_type.11
  2.0 1.0 %multiply_sine_fusion = (f32[32,520]{1,0:T(8,128)}, f32[32,520]{1,0:T(8,128)}) fusion(f32[520]{0:T(1024)S(1)} %pad_maximum_fusion, f32[32]{0:T(128)S(1)} %negate_power_fusion), kind=kLoop, calls=%fused_computation | loop fusion | flops 16640 | bytes 135328 | tf_op jit(solution)/shard_map/sin | solution.py:402
  3.0 0.0 copy-start.1
  3.0 0.0 copy-start.2
  3.0 0.0 copy-start.3
  3.0 0.0 copy-start.6
  3.0 0.0 copy-start.7
  3.0 13.1 %project.1 = (bf16[3,576,512]{2,1,0:T(8,128)(2,1)}, bf16[3,8,576]{2,1,0:T(8,128)(2,1)}) custom-call(f32[2304]{0:T(1024)} %gain_ref.2, f32[32,520]{1,0:T(8,128)} %get-tuple-element.13.cos_ref, f32[32,520]{1,0:T(8,128)} %get-tuple-element.12.sin_ref, bf16[512,2304]{1,0:T(8,128)(2,1)} %tok_hbm.3, bf16[8,2304]{1,0:T(8,128)(2,1)} %dtok_hbm.3, ...), custom_call_target="tpu_custom_call" | custom-call | tf_op jit(solution)/shard_map/project/pallas_call | solution.py:81
  16.2 0.0 copy-done.1
  16.2 0.0 copy-done.2
  16.2 0.0 copy-done.3
  16.2 0.0 copy-done.6
  16.2 0.0 copy-done.7
  16.2 0.0 copy-start
  16.2 1.5 %copy-done = bf16[3,576,512]{2,1,0:T(8,128)(2,1)S(1)} copy-done((bf16[3,576,512]{2,1,0:T(8,128)(2,1)S(1)}, bf16[3,576,512]{2,1,0:T(8,128)(2,1)}, u32[]{:S(2)}) %copy-start) | copy-done | bytes 1769496
  17.7 0.0 copy-start.4
  17.7 0.8 %copy-done.4 = bf16[3,8,576]{2,1,0:T(8,128)(2,1)S(1)} copy-done((bf16[3,8,576]{2,1,0:T(8,128)(2,1)S(1)}, bf16[3,8,576]{2,1,0:T(8,128)(2,1)}, u32[]{:S(2)}) %copy-start.4) | copy-done | bytes 27672
  18.5 0.0 copy-start.5
  18.5 44.6 %attention.1 = (bf16[512,2304]{1,0:T(8,128)(2,1)S(1)}, bf16[8,2304]{1,0:T(8,128)(2,1)S(1)}) custom-call(bf16[3,576,512]{2,1,0:T(8,128)(2,1)S(1)} %copy-done, bf16[3,8,576]{2,1,0:T(8,128)(2,1)S(1)} %copy-done.4, f32[32,520]{1,0:T(8,128)S(1)} %copy-done.2, f32[32,520]{1,0:T(8,128)S(1)} %copy-done.1, s32[64]{0:T(128)S(1)} %copy-done.7, s32[1]{0:T(128)S(6)} %copy.15.offset_ref, ...), custom_call_target="tpu_custom_call" | custom-call | tf_op jit(solution)/shard_map/attention/pallas_call | solution.py:321
  63.1 0.0 copy-done.5
  63.1 3.2 %final_norm.1 = (bf16[512,2304]{1,0:T(8,128)(2,1)}, bf16[8,2304]{1,0:T(8,128)(2,1)}, bf16[512,2304]{1,0:T(8,128)(2,1)}, bf16[8,2304]{1,0:T(8,128)(2,1)}) custom-call(f32[2304]{0:T(1024)S(1)} %copy-done.5, bf16[512,2304]{1,0:T(8,128)(2,1)S(1)} %get-tuple-element.10.in_ref, bf16[8,2304]{1,0:T(8,128)(2,1)S(1)} %get-tuple-element.11.din_ref), custom_call_target="tpu_custom_call" | custom-call | tf_op jit(solution)/shard_map/final_norm/pallas_call | solution.py:370
  (3 shorter events, 0.0 us)
Async XLA Ops:
  3.0 13.2 %copy-start.1 = (f32[32,520]{1,0:T(8,128)S(1)}, f32[32,520]{1,0:T(8,128)}, u32[]{:S(2)}) copy-start(f32[32,520]{1,0:T(8,128)} %get-tuple-element.12.sin_ref) | copy-start | bytes 199684
  3.0 13.2 %copy-start.2 = (f32[32,520]{1,0:T(8,128)S(1)}, f32[32,520]{1,0:T(8,128)}, u32[]{:S(2)}) copy-start(f32[32,520]{1,0:T(8,128)} %get-tuple-element.13.cos_ref) | copy-start | bytes 199684
  3.0 13.2 %copy-start.3 = (bf16[8,2304]{1,0:T(8,128)(2,1)S(1)}, bf16[8,2304]{1,0:T(8,128)(2,1)}, u32[]{:S(2)}) copy-start(bf16[8,2304]{1,0:T(8,128)(2,1)} %dtok_hbm.3) | copy-start | bytes 110596
  3.0 13.2 %copy-start.6 = (s32[8]{0:T(128)S(1)}, s32[8]{0:T(128)}, u32[]{:S(2)}) copy-start(s32[8]{0:T(128)} %length_ref.1) | copy-start | bytes 100
  3.0 13.2 %copy-start.7 = (s32[64]{0:T(128)S(1)}, s32[64]{0:T(128)}, u32[]{:S(2)}) copy-start(s32[64]{0:T(128)} %slot_ref.1) | copy-start | bytes 772
  16.2 1.5 %copy-start = (bf16[3,576,512]{2,1,0:T(8,128)(2,1)S(1)}, bf16[3,576,512]{2,1,0:T(8,128)(2,1)}, u32[]{:S(2)}) copy-start(bf16[3,576,512]{2,1,0:T(8,128)(2,1)} %get-tuple-element.8.proj_hbm) | copy-start | bytes 5308420
  17.7 0.8 %copy-start.4 = (bf16[3,8,576]{2,1,0:T(8,128)(2,1)S(1)}, bf16[3,8,576]{2,1,0:T(8,128)(2,1)}, u32[]{:S(2)}) copy-start(bf16[3,8,576]{2,1,0:T(8,128)(2,1)} %get-tuple-element.9.dec_hbm) | copy-start | bytes 82948
  18.5 44.7 %copy-start.5 = (f32[2304]{0:T(1024)S(1)}, f32[2304]{0:T(1024)}, u32[]{:S(2)}) copy-start(f32[2304]{0:T(1024)} %gain_ref.3) | copy-start | bytes 27652

commit v4 on v3

--- a/solution.py
+++ b/solution.py
@@ -42,26 +42,19 @@
 
 
 def project_kernel(
-    gain_ref, cos_ref, sin_ref, tok_hbm, dtok_hbm, w_hbm, out_ref, dec_ref,
-    tok, dtok, w, normed, dnormed, tok_sem, dtok_sem, w_sem,
+    gain_ref, cos_ref, sin_ref, tok, dtok, w_hbm, out_ref, dec_ref, w, normed, dnormed, w_sem,
 ):
     rows = tok.shape[0]
     loads = [pltpu.make_async_copy(w_hbm.at[part], w.at[part], w_sem.at[part]) for part in range(3)]
-    tok_load = pltpu.make_async_copy(tok_hbm, tok, tok_sem)
-    dtok_load = pltpu.make_async_copy(dtok_hbm, dtok, dtok_sem)
-    tok_load.start()
-    dtok_load.start()
     for load in loads:
         load.start()
     gain = gain_ref[...].reshape(1, gain_ref.shape[0])
-    tok_load.wait()
 
     @pl.loop(0, rows // 64)
     def _(i):
         span = pl.ds(pl.multiple_of(i * 64, 64), 64)
         normed[span, :] = rms_rows(tok[span, :].astype(F32), gain)
 
-    dtok_load.wait()
     dnormed[...] = rms_rows(dtok[...].astype(F32), gain)
     for part in range(3):
         loads[part].wait()
@@ -80,35 +73,31 @@
     local = w.shape[1]
     return pl.pallas_call(
         project_kernel,
-        in_specs=[VSPEC] * 3 + [HSPEC] * 3,
+        in_specs=[VSPEC] * 5 + [HSPEC],
         out_specs=[VSPEC] * 2,
         out_shape=[
             jax.ShapeDtypeStruct((3, local, rows), BF16),
             jax.ShapeDtypeStruct((3, drows, local), BF16),
         ],
         scratch_shapes=[
-            VMEM((rows, width), BF16),
-            VMEM((drows, width), BF16),
             VMEM((3, local, width), BF16),
             VMEM((rows, width), BF16),
             VMEM((drows, width), BF16),
-            pltpu.SemaphoreType.DMA(()),
-            pltpu.SemaphoreType.DMA(()),
             pltpu.SemaphoreType.DMA((3,)),
         ],
-        compiler_params=pltpu.CompilerParams(vmem_limit_bytes=59 * MIB),
+        compiler_params=pltpu.CompilerParams(vmem_limit_bytes=48 * MIB),
         name="project",
     )(gain, cosine, sine, tokens, decode_tokens, w)
 
 
 def attention_kernel(
-    n, proj_hbm, dec_hbm, cos_ref, sin_ref, slot_ref, offset_ref, length_ref,
+    n, proj_ref, dec_ref, cos_ref, sin_ref, slot_ref, offset_ref, length_ref,
     pcache_hbm, dcache_hbm, w_hbm, tok_hbm, dtok_hbm,
     hid_ref, dhid_ref,
-    arrived, results, routed, proj_ref, pcache, dcache, w, tok, dtok, att, part, got1, pair, got2, dec,
+    arrived, results, routed, pcache, dcache, w, tok, dtok, att, part, got1, pair, got2, dec,
     load_sem, send1, recv1, send2, recv2, s1, r1, s2, r2, s3, r3, sd, rd,
 ):
-    slots, local = arrived.shape[2:]
+    slots, local = dec_ref.shape[1:]
     heads = local // HEAD
     rows = tok.shape[0]
     pieces, chunk = part.shape[:2]
@@ -129,10 +118,6 @@
             ((pcache_hbm, pcache), (w_hbm, w), (dcache_hbm, dcache), (tok_hbm, tok), (dtok_hbm, dtok))
         )
     ]
-    dec_load = pltpu.make_async_copy(dec_hbm, arrived.at[seq], load_sem.at[5])
-    proj_load = pltpu.make_async_copy(proj_hbm, proj_ref, load_sem.at[6])
-    dec_load.start()
-    proj_load.start()
     for load in loads:
         load.start()
 
@@ -176,7 +161,7 @@
         send(dec.at[tp], dec.at[tp], sd.at[step], rd.at[step], lax.rem(tp + step, 4)) for step in range(1, 4)
     ]
 
-    dec_load.wait()
+    arrived[seq] = dec_ref[...]
     for copy in there:
         copy.start()
 
@@ -185,7 +170,6 @@
         pair[c] = (part[c, pl.ds(mine, own_rows)].astype(F32) + got1[c].astype(F32)).astype(BF16)
         second[c].start()
 
-    proj_load.wait()
     loads[0].wait()
     bias = jnp.where(lax.broadcasted_iota(jnp.int32, (1, keys), 1) < offset_ref[0], 0.0, NEGATIVE)
     for c in range(pieces):
@@ -320,14 +304,13 @@
     sem = pltpu.SemaphoreType.DMA((pieces,))
     return pl.pallas_call(
         functools.partial(attention_kernel, n),
-        in_specs=[HSPEC] * 2 + [VSPEC] * 3 + [SSPEC] * 2 + [HSPEC] * 5,
+        in_specs=[VSPEC] * 5 + [SSPEC] * 2 + [HSPEC] * 5,
         out_specs=[VSPEC] * 2,
         out_shape=[jax.ShapeDtypeStruct((rows, width), BF16), jax.ShapeDtypeStruct((slots, width), BF16)],
         scratch_shapes=[
             VMEM((n, 3, slots, local), BF16),
             VMEM((n, slots, local), BF16),
             VMEM((n * slots, local), F32),
-            VMEM(projected.shape, BF16),
             VMEM(pcache.shape, BF16),
             VMEM(dcache.shape, BF16),
             VMEM(w.shape, BF16),
@@ -337,7 +320,7 @@
             VMEM((pieces, chunk, width), BF16),
             buffer, buffer, buffer,
             VMEM((4, slots, width), BF16),
-            pltpu.SemaphoreType.DMA((7,)),
+            pltpu.SemaphoreType.DMA((5,)),
         ]
         + [pltpu.SemaphoreType.DMA((n,))] * 4
         + [sem] * 6

time: 66.6 us -> 61.8 us (0.928)
  Pallas kernels: 61 us -> 56 us
  local copies, waits for them, and re-layouts: 2.25 us -> 3.15 us
  other arithmetic: 1.72 us -> 1.05 us
    pallas_call x2, Pallas kernels: 57.8 us -> 52.8 us  [the longest x1 44.2 us: attention(): pl.pallas_call(functools.partial(attention_kernel, n), in_specs=[VSPEC] *...]
    unnamed x16 -> x12, local copies, waits for them, and re-layouts: 2.25 us -> 3.15 us
    sin x1, other arithmetic: 1.03 us -> 0.36 us  [local_step(): cosine, sine = (jnp.cos(angles), jnp.sin(angles))]
where the time goes in v4:
time: 61.8 us; the launch traced here: 61.6 us
  Pallas kernels  56 us (91%)
  local copies, waits for them, and re-layouts  3.15 us (5%)
  between operations  1.35 us (2%)
  other arithmetic  1.05 us (2%)
    pallas_call x1, Pallas kernels, attention(): pl.pallas_call(functools.partial(attention_kernel, n), in_specs=[VSPEC] *...  44.2 us
    pallas_call x1, Pallas kernels, project(): pl.pallas_call(project_kernel, in_specs=[VSPEC] * 5 + [HSPEC], out_specs=...  8.55 us
    pallas_call x1, Pallas kernels, final_norm(): pl.pallas_call(norm_kernel, grid=(rows // block,), in_specs=[pl.BlockSpec...  3.22 us
    unnamed x12, local copies, waits for them, and re-layouts  3.15 us

profile of v4, /device:TPU:0, one launch (start us, length us, event | category | flops | bytes accessed | tf_op | source)
XLA Modules:
  0.0 61.6 jit_solution(9425218155166880536)
XLA Ops:
  1.3 0.7 %convert_element_type.11 = f32[8]{0:T(128)S(1)} convert(s32[8]{0:T(128)} %length_ref.1) | non-fusion elementwise | flops 8 | bytes 64 | tf_op jit(solution)/shard_map/convert_element_type | solution.py:382
  2.0 0.4 multiply_sine_fusion
  2.3 0.0 copy-start
  2.4 1.7 %copy-done = bf16[512,2304]{1,0:T(8,128)(2,1)S(1)} copy-done((bf16[512,2304]{1,0:T(8,128)(2,1)S(1)}, bf16[512,2304]{1,0:T(8,128)(2,1)}, u32[]{:S(2)}) %copy-start) | copy-done | bytes 2359320
  4.0 0.0 copy-start.1
  4.0 0.8 %copy-done.1 = bf16[8,2304]{1,0:T(8,128)(2,1)S(1)} copy-done((bf16[8,2304]{1,0:T(8,128)(2,1)S(1)}, bf16[8,2304]{1,0:T(8,128)(2,1)}, u32[]{:S(2)}) %copy-start.1) | copy-done | bytes 36888
  4.8 0.0 copy-start.2
  4.8 0.7 %copy-done.2 = f32[2304]{0:T(1024)S(1)} copy-done((f32[2304]{0:T(1024)S(1)}, f32[2304]{0:T(1024)}, u32[]{:S(2)}) %copy-start.2) | copy-done | bytes 9240
  5.5 0.0 copy-start.4
  5.5 0.0 copy-start.5
  5.5 8.5 %project.1 = (bf16[3,576,512]{2,1,0:T(8,128)(2,1)S(1)}, bf16[3,8,576]{2,1,0:T(8,128)(2,1)S(1)}) custom-call(f32[2304]{0:T(1024)S(1)} %copy-done.2, f32[32,520]{1,0:T(8,128)S(1)} %get-tuple-element.13.cos_ref, f32[32,520]{1,0:T(8,128)S(1)} %get-tuple-element.12.sin_ref, bf16[512,2304]{1,0:T(8,128)(2,1)S(1)} %copy-done, bf16[8,2304]{1,0:T(8,128)(2,1)S(1)} %copy-done.1, ...), custom_call_target="tpu_custom_call" | custom-call | tf_op jit(solution)/shard_map/project/pallas_call | solution.py:74
  14.0 0.0 copy-done.4
  14.1 0.0 copy-done.5
  14.1 0.0 copy-start.3
  14.1 44.2 %attention.1 = (bf16[512,2304]{1,0:T(8,128)(2,1)S(1)}, bf16[8,2304]{1,0:T(8,128)(2,1)S(1)}) custom-call(bf16[3,576,512]{2,1,0:T(8,128)(2,1)S(1)} %get-tuple-element.8.proj_ref, bf16[3,8,576]{2,1,0:T(8,128)(2,1)S(1)} %get-tuple-element.9.dec_ref, f32[32,520]{1,0:T(8,128)S(1)} %get-tuple-element.13.cos_ref, f32[32,520]{1,0:T(8,128)S(1)} %get-tuple-element.12.sin_ref, ...), custom_call_target="tpu_custom_call" | custom-call | tf_op jit(solution)/shard_map/attention/pallas_call | solution.py:305
  58.3 0.0 copy-done.3
  58.3 3.2 %final_norm.1 = (bf16[512,2304]{1,0:T(8,128)(2,1)}, bf16[8,2304]{1,0:T(8,128)(2,1)}, bf16[512,2304]{1,0:T(8,128)(2,1)}, bf16[8,2304]{1,0:T(8,128)(2,1)}) custom-call(f32[2304]{0:T(1024)S(1)} %copy-done.3, bf16[512,2304]{1,0:T(8,128)(2,1)S(1)} %get-tuple-element.10.in_ref, bf16[8,2304]{1,0:T(8,128)(2,1)S(1)} %get-tuple-element.11.din_ref), custom_call_target="tpu_custom_call" | custom-call | tf_op jit(solution)/shard_map/final_norm/pallas_call | solution.py:353
  (3 shorter events, 0.0 us)
Async XLA Ops:
  2.3 1.7 %copy-start = (bf16[512,2304]{1,0:T(8,128)(2,1)S(1)}, bf16[512,2304]{1,0:T(8,128)(2,1)}, u32[]{:S(2)}) copy-start(bf16[512,2304]{1,0:T(8,128)(2,1)} %tok_hbm.1) | copy-start | bytes 7077892
  4.0 0.8 %copy-start.1 = (bf16[8,2304]{1,0:T(8,128)(2,1)S(1)}, bf16[8,2304]{1,0:T(8,128)(2,1)}, u32[]{:S(2)}) copy-start(bf16[8,2304]{1,0:T(8,128)(2,1)} %dtok_hbm.1) | copy-start | bytes 110596
  4.8 0.7 %copy-start.2 = (f32[2304]{0:T(1024)S(1)}, f32[2304]{0:T(1024)}, u32[]{:S(2)}) copy-start(f32[2304]{0:T(1024)} %gain_ref.2) | copy-start | bytes 27652
  5.5 8.6 %copy-start.4 = (s32[8]{0:T(128)S(1)}, s32[8]{0:T(128)}, u32[]{:S(2)}) copy-start(s32[8]{0:T(128)} %length_ref.1) | copy-start | bytes 100
  5.5 8.6 %copy-start.5 = (s32[64]{0:T(128)S(1)}, s32[64]{0:T(128)}, u32[]{:S(2)}) copy-start(s32[64]{0:T(128)} %slot_ref.1) | copy-start | bytes 772
  14.1 44.3 %copy-start.3 = (f32[2304]{0:T(1024)S(1)}, f32[2304]{0:T(1024)}, u32[]{:S(2)}) copy-start(f32[2304]{0:T(1024)} %gain_ref.3) | copy-start | bytes 27652
